TPU v7x, 32 devices: a whole 2x2x4 slice. The times are simulated.
32 devices in a mesh: lat: 4 (over y, x), lon: 8 (over z, core).
Axes of the slice: x: 2, y: 2, z: 4, core: 2. Of those that a mesh axis runs over, the one named last changes fastest.
Arguments:
- grad_rows: bfloat16 [32768, 128], P(('lat', 'lon')), may hold values from -6 to 6
- owner: int32 [32768, 1], P(('lat', 'lon')), may hold values from 0 to 31; in each aligned block of 1024 rows (0 to 1023, 1024 to 2047, ...) at most 64 rows name the same one
- lat_offset: int32 [32768], P(('lat', 'lon')), may hold values from 0 to 63
- lon_offset: int32 [32768], P(('lat', 'lon')), may hold values from 0 to 127
- position: bfloat16 [32768, 2], P(('lat', 'lon')), may hold values from 0 to 1
- live_count: int32 [32], P(('lat', 'lon')), may hold values from 512 to 1024
- features: bfloat16 [256, 1024, 128], P('lat', 'lon'), may hold values from -6 to 6
- conv_weight: bfloat16 [3, 3, 128, 128], replicated, may hold values from -0.1875 to 0.1875
Outputs:
- input_grad: bfloat16 [256, 1024, 128], P('lat', 'lon')
- weight_grad: float32 [3, 3, 128, 128], replicated
Inputs may be any that keep to these rules, and one draw needn't show every extreme that they name: `owner`: among the 1024 rows of one device no tile is named more than 64 times, a bound that some block reaches. `live_count`: entry k counts the real rows among the rows of device k, which come first.
All inputs are finite; a program needn't handle non-finite values.
Results may differ from a plain program's by a relative error of at most 0.012.
Values may be sent and summed in bfloat16 or wider, within the bound.
A program may use at most 128 MiB of HBM per device.

v0:
```python
import math

import jax
import jax.numpy as jnp
from jax import lax
from jax.sharding import PartitionSpec as P

rbf_scale = 1.5


def padded_2(cells, sides, width, closed):
    for axis, dim in sides:
        count = lax.axis_size(axis)
        ends = count if closed else count - 1
        head = lax.slice_in_dim(cells, 0, width, axis=dim)
        tail = lax.slice_in_dim(cells, cells.shape[dim] - width, cells.shape[dim], axis=dim)
        cells = jnp.concatenate(
            [
                lax.ppermute(tail, axis, [(i, (i + 1) % count) for i in range(ends)]),
                cells,
                lax.ppermute(head, axis, [((i + 1) % count, i) for i in range(ends)]),
            ],
            axis=dim,
        )
    return cells


def profile(frac):
    tap_index = jnp.arange(8).astype(frac.dtype)
    return jnp.exp(
        -jnp.square(tap_index[None, :] - 3.0 - frac[:, None]) / (2.0 * rbf_scale * rbf_scale)
    )


def clear_rim(padded):
    lat_index = lax.axis_index("lat")
    lat_count = lax.axis_size("lat")
    row_line = jnp.arange(padded.shape[0], dtype=jnp.int32)
    masked = (row_line == 0) & (lat_index == 0) | (row_line == padded.shape[0] - 1) & (
        lat_index == lat_count - 1
    )
    return jnp.where(masked[:, None, None], jnp.zeros_like(padded), padded)


def tap_matrix(offsets, weights, extent):
    tap_ints = jnp.arange(8, dtype=jnp.int32)
    cells = offsets[:, None] + tap_ints[None, :] + 1
    line = jnp.arange(extent, dtype=jnp.int32)
    picked = jnp.where(
        cells[:, :, None] == line[None, None, :], weights.astype(jnp.float32)[:, :, None], 0.0
    )
    return jnp.sum(picked, axis=1).astype(jnp.bfloat16)


def shards(grad_rows, owner, lat_offset, lon_offset, position, live_count, features, conv_weight):
    lat_total = lax.axis_size("lat")
    lon_total = lax.axis_size("lon")
    device_total = lat_total * lon_total
    row_total = grad_rows.shape[0]
    channels = grad_rows.shape[1]
    tile_lat = features.shape[0]
    tile_lon = features.shape[1]
    capacity = max(2, 2 * row_total // device_total)
    input_padded = clear_rim(padded_2(features, (("lat", 0), ("lon", 1)), 1, True))
    owner_tile = owner[:, 0]
    is_live = jnp.arange(row_total, dtype=jnp.int32) < live_count[0]
    matches = (
        (owner_tile[:, None] == jnp.arange(device_total, dtype=jnp.int32)[None, :])
        & is_live[:, None]
    ).astype(jnp.int32)
    earlier = jnp.cumsum(matches, axis=0) - matches
    slot_rank = jnp.sum(earlier * matches, axis=1)
    slot_index = jnp.where(is_live, owner_tile * capacity + slot_rank, device_total * capacity)
    outgoing = (
        jnp.zeros((device_total * capacity, channels), jnp.bfloat16)
        .at[slot_index]
        .set(grad_rows, mode="drop")
    )
    geometry = jnp.stack(
        [
            position[:, 0],
            position[:, 1],
            lat_offset.astype(jnp.bfloat16),
            lon_offset.astype(jnp.bfloat16),
        ],
        axis=1,
    )
    place_out = (
        jnp.zeros((device_total * capacity, 4), jnp.bfloat16)
        .at[slot_index]
        .set(geometry, mode="drop")
    )
    incoming, place_in = (
        lax.all_to_all(
            outgoing.reshape(device_total, capacity, channels),
            ("lat", "lon"),
            split_axis=0,
            concat_axis=0,
            tiled=True,
        ),
        lax.all_to_all(
            place_out.reshape(device_total, capacity, 4),
            ("lat", "lon"),
            split_axis=0,
            concat_axis=0,
            tiled=True,
        ),
    )
    incoming = incoming.reshape(-1, channels)
    place_in = place_in.reshape(-1, 4).astype(jnp.float32)
    padded_lat = tile_lat + 8
    padded_lon = tile_lon + 8
    slot_total = incoming.shape[0]
    block_rows = math.gcd(slot_total, 256)

    def accumulate(canvas, payload):
        rows_blk, place_blk = payload
        lat_weight = profile(place_blk[:, 0]).astype(jnp.bfloat16)
        lon_weight = profile(place_blk[:, 1]).astype(jnp.bfloat16)
        lat_matrix = tap_matrix(place_blk[:, 2].astype(jnp.int32), lat_weight, padded_lat)
        lon_matrix = tap_matrix(place_blk[:, 3].astype(jnp.int32), lon_weight, padded_lon)
        spread = (lon_matrix[:, :, None] * rows_blk[:, None, :]).reshape(
            rows_blk.shape[0], padded_lon * channels
        )
        canvas = canvas + lax.dot_general(
            lat_matrix, spread, (((0,), (0,)), ((), ())), preferred_element_type=jnp.float32
        )
        return (canvas, None)

    canvas, _ = lax.scan(
        accumulate,
        jnp.zeros((padded_lat, padded_lon * channels), jnp.float32),
        (incoming.reshape(-1, block_rows, channels), place_in.reshape(-1, block_rows, 4)),
    )
    canvas = canvas.reshape(padded_lat, padded_lon, channels)
    edge_rows = jnp.concatenate([canvas[:5], canvas[-5:]], axis=0)
    edge_rows = padded_2(edge_rows.astype(jnp.bfloat16), (("lat", 0),), 5, False).astype(
        edge_rows.dtype
    )
    inner = canvas[4:-4]
    inner = inner.at[:4].add(edge_rows[1:5]).at[-4:].add(edge_rows[15:19])
    rim_top = edge_rows[0] + canvas[3]
    rim_bottom = canvas[-4] + edge_rows[19]
    tall = jnp.concatenate([rim_top[None], inner, rim_bottom[None]], axis=0)
    side_cols = jnp.concatenate([tall[:, :5], tall[:, -5:]], axis=1)
    side_cols = padded_2(side_cols.astype(jnp.bfloat16), (("lon", 1),), 5, True).astype(
        side_cols.dtype
    )
    middle = tall[:, 4:-4]
    middle = middle.at[:, :4].add(side_cols[:, 1:5]).at[:, -4:].add(side_cols[:, 15:19])
    rim_left = side_cols[:, 0] + tall[:, 3]
    rim_right = tall[:, -4] + side_cols[:, 19]
    whole = jnp.concatenate([rim_left[:, None], middle, rim_right[:, None]], axis=1)
    grid_padded = clear_rim(whole.astype(jnp.bfloat16))
    grid_grad = grid_padded[1:-1, 1:-1]
    flat_grad = grid_grad.reshape(-1, channels)
    input_grad = jnp.zeros((tile_lat * tile_lon, channels), jnp.float32)
    weight_parts = []
    for a in range(3):
        for b in range(3):
            shifted = grid_padded[2 - a : 2 - a + tile_lat, 2 - b : 2 - b + tile_lon].reshape(
                -1, channels
            )
            input_grad = input_grad + lax.dot_general(
                shifted,
                conv_weight[a, b],
                (((1,), (1,)), ((), ())),
                preferred_element_type=jnp.float32,
            )
            window = input_padded[a : a + tile_lat, b : b + tile_lon].reshape(-1, channels)
            weight_parts.append(
                lax.dot_general(
                    window, flat_grad, (((0,), (0,)), ((), ())), preferred_element_type=jnp.float32
                )
            )
    weight_grad = lax.psum(
        jnp.stack(weight_parts).reshape(3, 3, channels, channels), ("lat", "lon")
    )
    return (input_grad.reshape(tile_lat, tile_lon, channels).astype(jnp.bfloat16), weight_grad)


def solution(mesh):
    placed = (
        P(("lat", "lon"), None),
        P(("lat", "lon"), None),
        P(("lat", "lon")),
        P(("lat", "lon")),
        P(("lat", "lon"), None),
        P(("lat", "lon")),
        P("lat", "lon", None),
        P(),
    )
    return jax.shard_map(
        shards, mesh=mesh, in_specs=placed, out_specs=(P("lat", "lon", None), P()), check_vma=False
    )
```

profile of v0, /device:TPU:0, one launch (start us, length us, event | category | flops | bytes accessed | tf_op | source)
XLA Modules:
  0.0 337.5 jit_solution(12751207130138029418)
XLA Ops:
  9.9 9.0 %reduce-window.6 = s32[32,8,128]{2,1,0:T(8,128)S(1)} reduce-window(s32[32,8,128]{2,1,0:T(8,128)S(1)} %fusion.91, s32[]{:T(128)} %constant.163.clone.1), window={size=1x1x128 pad=0_0x0_0x127_0}, to_apply=%region_0.1 | reduce-window | flops 4161536 | bytes 262148 | tf_op jit(solution)/shard_map/reduce-window
  21.8 3.3 scatter_custom_fusion
  26.1 7.3 %all-to-all-start = ((bf16[32,2,128]{2,1,0:T(2,128)(2,1)}), bf16[32,2,128]{2,1,0:T(2,128)(2,1)S(1)}, u32[]{:S(2)}, u32[]{:S(2)}) async-start(bf16[32,2,128]{2,1,0:T(2,128)(2,1)} %reshape.426), calls=%async_computation | async-start | bytes 32768 | tf_op jit(solution)/shard_map/all_to_all | solution.py:101
  33.4 4.3 %scatter_custom_fusion.1 = bf16[2048,128]{1,0:T(8,128)(2,1)} fusion(s32[1024]{0:T(1024)S(1)} %bitcast.220, bf16[1024,128]{1,0:T(8,128)(2,1)} %param.18, bf16[]{:T(256)} %constant.167.clone.1), kind=kCustom, calls=%fused_computation.79 | custom fusion | bytes 524800 | tf_op jit(solution)/shard_map/scatter | solution.py:77
  37.8 2.8 all-to-all-done
  40.5 3.1 all-to-all-start.1
  47.3 5.0 %collective-permute-done.4 = bf16[1,128,128]{2,1,0:T(8,128)(2,1)S(1)} collective-permute-done((bf16[1,128,128]{2,1,0:T(8,128)(2,1)S(1)}, bf16[1,128,128]{2,1,0:T(8,128)(2,1)S(1)}, u32[]{:S(2)}, u32[]{:S(2)}) %collective-permute-start.4) | collective-permute-done | bytes 32800 | tf_op jit(solution)/shard_map/ppermute | solution.py:19
  54.4 3.5 %collective-permute-start.7 = (bf16[66,1,128]{2,1,0:T(2,128)(2,1)S(1)}, bf16[66,1,128]{2,1,0:T(2,128)(2,1)S(1)}, u32[]{:S(2)}, u32[]{:S(2)}) collective-permute-start(bf16[66,1,128]{2,1,0:T(2,128)(2,1)S(1)} %get-tuple-element.167), channel_id=1, source_target_pairs={{1,0},{2,1},{3,2},{4,3},{5,4},{6,5},{7,6},{0,7},{9,8},{10,9},{11,1... | collective-permute-start | bytes 50696 | tf_op jit(solution)/shard_map/ppermute | solution.py:21
  60.2 92.0 %while.17 = (s32[]{:T(128)}, f32[72,17408]{1,0:T(8,128)}, f32[8,256,4]{1,0,2:T(8,128)S(1)}, bf16[8,256,128]{2,1,0:T(8,128)(2,1)S(1)}, s32[]{:T(128)}, /*index=5*/s32[]{:T(128)}) while((s32[]{:T(128)}, f32[72,17408]{1,0:T(8,128)}, f32[8,256,4]{1,0,2:T(8,128)S(1)}, bf16[8,256,128]{2,1,0:T(8,128)(2,1)S(1)}, s32[]{:T(128)}, ...), condition=%wide.region_8.9_spmd.clone, body=%wide.region_5.8_spmd.clone.sunk | while | flops 649949696 | bytes 63590632 | solution.py:130
  60.7 5.2 %broadcast_multiply_fusion.2 = bf16[256,136,128]{2,1,0:T(8,128)(2,1)S(1)} fusion(bf16[256,128]{1,0:T(8,128)(2,1)S(1)} %dynamic-slice_bitcast_fusion.2, bf16[256,136]{1,0:T(8,128)(2,1)S(1)} %copy.114), kind=kLoop, calls=%fused_computation.5.clone.1 | loop fusion | flops 4456448 | bytes 9048064 | tf_op jit(solution)/shard_map/while/body/eval_jaxpr/mul | solution.py:122
  65.9 3.6 %convolution_add_fusion.10 = f32[72,17408]{1,0:T(8,128)S(1)} fusion(bf16[32,8,136,128]{3,2,1,0:T(8,128)(2,1)S(1)} %bitcast.180, f32[72,17408]{1,0:T(8,128)S(1)} %bitcast.182, pred[]{:T(512)S(6)} %compare.25, bf16[256,72]{0,1:T(8,128)(2,1)S(1)} %select_reduce_fusion.5), kind=kOutput, calls=%fused_computation.2.clone.1 | convolution fusion | flops 644235264 | bytes 18976768 | tf_op jit(solution)/shard_map/while/body/eval_jaxpr/dot_general | solution.py:125
  72.2 5.2 %broadcast_multiply_fusion.2 = bf16[256,136,128]{2,1,0:T(8,128)(2,1)S(1)} fusion(bf16[256,128]{1,0:T(8,128)(2,1)S(1)} %dynamic-slice_bitcast_fusion.2, bf16[256,136]{1,0:T(8,128)(2,1)S(1)} %copy.114), kind=kLoop, calls=%fused_computation.5.clone.1 | loop fusion | flops 4456448 | bytes 9048064 | tf_op jit(solution)/shard_map/while/body/eval_jaxpr/mul | solution.py:122
  77.4 3.6 %convolution_add_fusion.10 = f32[72,17408]{1,0:T(8,128)S(1)} fusion(bf16[32,8,136,128]{3,2,1,0:T(8,128)(2,1)S(1)} %bitcast.180, f32[72,17408]{1,0:T(8,128)S(1)} %bitcast.182, pred[]{:T(512)S(6)} %compare.25, bf16[256,72]{0,1:T(8,128)(2,1)S(1)} %select_reduce_fusion.5), kind=kOutput, calls=%fused_computation.2.clone.1 | convolution fusion | flops 644235264 | bytes 18976768 | tf_op jit(solution)/shard_map/while/body/eval_jaxpr/dot_general | solution.py:125
  83.7 5.2 %broadcast_multiply_fusion.2 = bf16[256,136,128]{2,1,0:T(8,128)(2,1)S(1)} fusion(bf16[256,128]{1,0:T(8,128)(2,1)S(1)} %dynamic-slice_bitcast_fusion.2, bf16[256,136]{1,0:T(8,128)(2,1)S(1)} %copy.114), kind=kLoop, calls=%fused_computation.5.clone.1 | loop fusion | flops 4456448 | bytes 9048064 | tf_op jit(solution)/shard_map/while/body/eval_jaxpr/mul | solution.py:122
  88.9 3.6 %convolution_add_fusion.10 = f32[72,17408]{1,0:T(8,128)S(1)} fusion(bf16[32,8,136,128]{3,2,1,0:T(8,128)(2,1)S(1)} %bitcast.180, f32[72,17408]{1,0:T(8,128)S(1)} %bitcast.182, pred[]{:T(512)S(6)} %compare.25, bf16[256,72]{0,1:T(8,128)(2,1)S(1)} %select_reduce_fusion.5), kind=kOutput, calls=%fused_computation.2.clone.1 | convolution fusion | flops 644235264 | bytes 18976768 | tf_op jit(solution)/shard_map/while/body/eval_jaxpr/dot_general | solution.py:125
  95.2 5.2 %broadcast_multiply_fusion.2 = bf16[256,136,128]{2,1,0:T(8,128)(2,1)S(1)} fusion(bf16[256,128]{1,0:T(8,128)(2,1)S(1)} %dynamic-slice_bitcast_fusion.2, bf16[256,136]{1,0:T(8,128)(2,1)S(1)} %copy.114), kind=kLoop, calls=%fused_computation.5.clone.1 | loop fusion | flops 4456448 | bytes 9048064 | tf_op jit(solution)/shard_map/while/body/eval_jaxpr/mul | solution.py:122
  100.4 3.6 %convolution_add_fusion.10 = f32[72,17408]{1,0:T(8,128)S(1)} fusion(bf16[32,8,136,128]{3,2,1,0:T(8,128)(2,1)S(1)} %bitcast.180, f32[72,17408]{1,0:T(8,128)S(1)} %bitcast.182, pred[]{:T(512)S(6)} %compare.25, bf16[256,72]{0,1:T(8,128)(2,1)S(1)} %select_reduce_fusion.5), kind=kOutput, calls=%fused_computation.2.clone.1 | convolution fusion | flops 644235264 | bytes 18976768 | tf_op jit(solution)/shard_map/while/body/eval_jaxpr/dot_general | solution.py:125
  106.7 5.2 %broadcast_multiply_fusion.2 = bf16[256,136,128]{2,1,0:T(8,128)(2,1)S(1)} fusion(bf16[256,128]{1,0:T(8,128)(2,1)S(1)} %dynamic-slice_bitcast_fusion.2, bf16[256,136]{1,0:T(8,128)(2,1)S(1)} %copy.114), kind=kLoop, calls=%fused_computation.5.clone.1 | loop fusion | flops 4456448 | bytes 9048064 | tf_op jit(solution)/shard_map/while/body/eval_jaxpr/mul | solution.py:122
  111.9 3.6 %convolution_add_fusion.10 = f32[72,17408]{1,0:T(8,128)S(1)} fusion(bf16[32,8,136,128]{3,2,1,0:T(8,128)(2,1)S(1)} %bitcast.180, f32[72,17408]{1,0:T(8,128)S(1)} %bitcast.182, pred[]{:T(512)S(6)} %compare.25, bf16[256,72]{0,1:T(8,128)(2,1)S(1)} %select_reduce_fusion.5), kind=kOutput, calls=%fused_computation.2.clone.1 | convolution fusion | flops 644235264 | bytes 18976768 | tf_op jit(solution)/shard_map/while/body/eval_jaxpr/dot_general | solution.py:125
  118.2 5.2 %broadcast_multiply_fusion.2 = bf16[256,136,128]{2,1,0:T(8,128)(2,1)S(1)} fusion(bf16[256,128]{1,0:T(8,128)(2,1)S(1)} %dynamic-slice_bitcast_fusion.2, bf16[256,136]{1,0:T(8,128)(2,1)S(1)} %copy.114), kind=kLoop, calls=%fused_computation.5.clone.1 | loop fusion | flops 4456448 | bytes 9048064 | tf_op jit(solution)/shard_map/while/body/eval_jaxpr/mul | solution.py:122
  123.4 3.6 %convolution_add_fusion.10 = f32[72,17408]{1,0:T(8,128)S(1)} fusion(bf16[32,8,136,128]{3,2,1,0:T(8,128)(2,1)S(1)} %bitcast.180, f32[72,17408]{1,0:T(8,128)S(1)} %bitcast.182, pred[]{:T(512)S(6)} %compare.25, bf16[256,72]{0,1:T(8,128)(2,1)S(1)} %select_reduce_fusion.5), kind=kOutput, calls=%fused_computation.2.clone.1 | convolution fusion | flops 644235264 | bytes 18976768 | tf_op jit(solution)/shard_map/while/body/eval_jaxpr/dot_general | solution.py:125
  129.7 5.2 %broadcast_multiply_fusion.2 = bf16[256,136,128]{2,1,0:T(8,128)(2,1)S(1)} fusion(bf16[256,128]{1,0:T(8,128)(2,1)S(1)} %dynamic-slice_bitcast_fusion.2, bf16[256,136]{1,0:T(8,128)(2,1)S(1)} %copy.114), kind=kLoop, calls=%fused_computation.5.clone.1 | loop fusion | flops 4456448 | bytes 9048064 | tf_op jit(solution)/shard_map/while/body/eval_jaxpr/mul | solution.py:122
  134.9 3.6 %convolution_add_fusion.10 = f32[72,17408]{1,0:T(8,128)S(1)} fusion(bf16[32,8,136,128]{3,2,1,0:T(8,128)(2,1)S(1)} %bitcast.180, f32[72,17408]{1,0:T(8,128)S(1)} %bitcast.182, pred[]{:T(512)S(6)} %compare.25, bf16[256,72]{0,1:T(8,128)(2,1)S(1)} %select_reduce_fusion.5), kind=kOutput, calls=%fused_computation.2.clone.1 | convolution fusion | flops 644235264 | bytes 18976768 | tf_op jit(solution)/shard_map/while/body/eval_jaxpr/dot_general | solution.py:125
  141.2 5.2 %broadcast_multiply_fusion.2 = bf16[256,136,128]{2,1,0:T(8,128)(2,1)S(1)} fusion(bf16[256,128]{1,0:T(8,128)(2,1)S(1)} %dynamic-slice_bitcast_fusion.2, bf16[256,136]{1,0:T(8,128)(2,1)S(1)} %copy.114), kind=kLoop, calls=%fused_computation.5.clone.1 | loop fusion | flops 4456448 | bytes 9048064 | tf_op jit(solution)/shard_map/while/body/eval_jaxpr/mul | solution.py:122
  146.4 3.6 %convolution_add_fusion.10 = f32[72,17408]{1,0:T(8,128)S(1)} fusion(bf16[32,8,136,128]{3,2,1,0:T(8,128)(2,1)S(1)} %bitcast.180, f32[72,17408]{1,0:T(8,128)S(1)} %bitcast.182, pred[]{:T(512)S(6)} %compare.25, bf16[256,72]{0,1:T(8,128)(2,1)S(1)} %select_reduce_fusion.5), kind=kOutput, calls=%fused_computation.2.clone.1 | convolution fusion | flops 644235264 | bytes 18976768 | tf_op jit(solution)/shard_map/while/body/eval_jaxpr/dot_general | solution.py:125
  153.6 2.8 convert.24
  160.1 4.6 %collective-permute-start = (bf16[5,136,128]{2,1,0:T(8,128)(2,1)S(1)}, bf16[5,136,128]{2,1,0:T(8,128)(2,1)S(1)}, u32[]{:S(2)}, u32[]{:S(2)}) collective-permute-start(bf16[5,136,128]{2,1,0:T(8,128)(2,1)S(1)} %bitcast.193), channel_id=1, source_target_pairs={{0,8},{8,16},{16,24},{1,9},{9,17},{17,25},{2,10},{10,18},{18,26},{... | collective-permute-start | bytes 522248 | tf_op jit(solution)/shard_map/ppermute | solution.py:19
  164.7 2.7 collective-permute-done.1
  168.9 3.5 %collective-permute-start.3 = (bf16[66,5,128]{2,1,0:T(8,128)(2,1)S(1)}, bf16[66,5,128]{2,1,0:T(8,128)(2,1)S(1)}, u32[]{:S(2)}, u32[]{:S(2)}) collective-permute-start(bf16[66,5,128]{2,1,0:T(8,128)(2,1)S(1)} %get-tuple-element.165), channel_id=1, source_target_pairs={{1,0},{2,1},{3,2},{4,3},{5,4},{6,5},{7,6},{0,7},{9,8},{10,9},{11,1... | collective-permute-start | bytes 253448 | tf_op jit(solution)/shard_map/ppermute | solution.py:21
  176.4 3.1 maximum_select_fusion.1
  179.5 7.0 %fusion.126 = (bf16[64,128,128]{2,1,0:T(8,128)(2,1)}, bf16[64,128,128]{2,1,0:T(8,128)(2,1)S(1)}, bf16[64,128,128]{2,1,0:T(8,128)(2,1)}, bf16[64,128,128]{2,1,0:T...) fusion(bf16[66,130,128]{2,1,0:T(8,128)(2,1)S(1)} %get-tuple-ele, ...), kind=kLoop, calls=%fused_computation.152 | loop fusion | bytes 37748736 | tf_op jit(solution)/shard_map/slice | solution.py:161
  212.8 116.0 %all-reduce.2.cloned.1.call-done = f32[3,3,128,128]{3,2,1,0:T(8,128)} async-done(((f32[3,3,128,128]{3,2,1,0:T(8,128)}), f32[3,3,128,128]{3,2,1,0:T(8,128)}) %all-reduce.2.cloned.1.call-update) | async-done | bytes 589840 | tf_op jit(solution)/shard_map/psum | solution.py:176
  (244 shorter events, 73.5 us)
Async XLA Ops:
  26.1 14.4 %all-to-all-start = ((bf16[32,2,128]{2,1,0:T(2,128)(2,1)}), bf16[32,2,128]{2,1,0:T(2,128)(2,1)S(1)}, u32[]{:S(2)}, u32[]{:S(2)}) async-start(bf16[32,2,128]{2,1,0:T(2,128)(2,1)} %reshape.426), calls=%async_computation | async-start | bytes 32768 | tf_op jit(solution)/shard_map/all_to_all | solution.py:101
  40.5 19.7 %all-to-all-start.1 = ((bf16[32,64,128]{2,1,0:T(8,128)(2,1)}), bf16[32,64,128]{2,1,0:T(8,128)(2,1)S(1)}, u32[]{:S(2)}, u32[]{:S(2)}) async-start(bf16[32,64,128]{2,1,0:T(8,128)(2,1)} %bitcast.8), calls=%async_computation.1 | async-start | bytes 1048576 | tf_op jit(solution)/shard_map/all_to_all | solution.py:94
  43.6 285.1 %all-reduce.2.cloned.1.call-start = ((), (), s32[]{:S(2)}) async-start(), calls=%async_computation.2 | async-start | bytes 1179648 | tf_op jit(solution)/shard_map/psum | solution.py:176
  44.4 9.8 %collective-permute-start.5 = (bf16[1,128,128]{2,1,0:T(8,128)(2,1)S(1)}, bf16[1,128,128]{2,1,0:T(8,128)(2,1)S(1)}, u32[]{:S(2)}, u32[]{:S(2)}) collective-permute-start(bf16[1,128,128]{2,1,0:T(8,128)(2,1)S(1)} %get-tuple-element.168), channel_id=1, source_target_pairs={{8,0},{16,8},{24,16},{0,24},{9,1},{17,9},{25,17},{1,25},{10,2},{18... | collective-permute-start | bytes 98312 | tf_op jit(solution)/shard_map/ppermute | solution.py:21
  47.1 5.2 %collective-permute-start.4 = (bf16[1,128,128]{2,1,0:T(8,128)(2,1)S(1)}, bf16[1,128,128]{2,1,0:T(8,128)(2,1)S(1)}, u32[]{:S(2)}, u32[]{:S(2)}) collective-permute-start(bf16[1,128,128]{2,1,0:T(8,128)(2,1)S(1)} %get-tuple-element.169), channel_id=1, source_target_pairs={{0,8},{8,16},{16,24},{24,0},{1,9},{9,17},{17,25},{25,1},{2,10},{10... | collective-permute-start | bytes 98312 | tf_op jit(solution)/shard_map/ppermute | solution.py:19
  54.3 122.0 %collective-permute-start.6 = (bf16[66,1,128]{2,1,0:T(2,128)(2,1)S(1)}, bf16[66,1,128]{2,1,0:T(2,128)(2,1)S(1)}, u32[]{:S(2)}, u32[]{:S(2)}) collective-permute-start(bf16[66,1,128]{2,1,0:T(2,128)(2,1)S(1)} %get-tuple-element.166), channel_id=1, source_target_pairs={{0,1},{1,2},{2,3},{3,4},{4,5},{5,6},{6,7},{7,0},{8,9},{9,10},{10,1... | collective-permute-start | bytes 50696 | tf_op jit(solution)/shard_map/ppermute | solution.py:19
  54.4 121.9 %collective-permute-start.7 = (bf16[66,1,128]{2,1,0:T(2,128)(2,1)S(1)}, bf16[66,1,128]{2,1,0:T(2,128)(2,1)S(1)}, u32[]{:S(2)}, u32[]{:S(2)}) collective-permute-start(bf16[66,1,128]{2,1,0:T(2,128)(2,1)S(1)} %get-tuple-element.167), channel_id=1, source_target_pairs={{1,0},{2,1},{3,2},{4,3},{5,4},{6,5},{7,6},{0,7},{9,8},{10,9},{11,1... | collective-permute-start | bytes 50696 | tf_op jit(solution)/shard_map/ppermute | solution.py:21
  60.6 5.2 %slice-start = ((s8[5013504]{0:T(1024)(128)(4,1)}), s8[4194304]{0:T(1024)(128)(4,1)S(1)}, s32[]{:S(2)}) async-start(s8[5013504]{0:T(1024)(128)(4,1)} %bitcast.181), calls=%async_computation.3 | async-start | bytes 8388608 | tf_op jit(solution)/shard_map/while
  60.7 5.2 %slice-start.1 = ((s8[5013504]{0:T(1024)(128)(4,1)}), s8[819200]{0:T(1024)(128)(4,1)S(1)}, s32[]{:S(2)}) async-start(s8[5013504]{0:T(1024)(128)(4,1)} %bitcast.181), calls=%async_computation.4 | async-start | bytes 1638400 | tf_op jit(solution)/shard_map/while
  69.5 2.2 copy-start
  72.2 5.2 %slice-start = ((s8[5013504]{0:T(1024)(128)(4,1)}), s8[4194304]{0:T(1024)(128)(4,1)S(1)}, s32[]{:S(2)}) async-start(s8[5013504]{0:T(1024)(128)(4,1)} %bitcast.181), calls=%async_computation.3 | async-start | bytes 8388608 | tf_op jit(solution)/shard_map/while
  72.2 5.2 %slice-start.1 = ((s8[5013504]{0:T(1024)(128)(4,1)}), s8[819200]{0:T(1024)(128)(4,1)S(1)}, s32[]{:S(2)}) async-start(s8[5013504]{0:T(1024)(128)(4,1)} %bitcast.181), calls=%async_computation.4 | async-start | bytes 1638400 | tf_op jit(solution)/shard_map/while
  81.0 2.2 copy-start
  83.7 5.2 %slice-start = ((s8[5013504]{0:T(1024)(128)(4,1)}), s8[4194304]{0:T(1024)(128)(4,1)S(1)}, s32[]{:S(2)}) async-start(s8[5013504]{0:T(1024)(128)(4,1)} %bitcast.181), calls=%async_computation.3 | async-start | bytes 8388608 | tf_op jit(solution)/shard_map/while
  83.7 5.2 %slice-start.1 = ((s8[5013504]{0:T(1024)(128)(4,1)}), s8[819200]{0:T(1024)(128)(4,1)S(1)}, s32[]{:S(2)}) async-start(s8[5013504]{0:T(1024)(128)(4,1)} %bitcast.181), calls=%async_computation.4 | async-start | bytes 1638400 | tf_op jit(solution)/shard_map/while
  92.5 2.2 copy-start
  95.2 5.2 %slice-start = ((s8[5013504]{0:T(1024)(128)(4,1)}), s8[4194304]{0:T(1024)(128)(4,1)S(1)}, s32[]{:S(2)}) async-start(s8[5013504]{0:T(1024)(128)(4,1)} %bitcast.181), calls=%async_computation.3 | async-start | bytes 8388608 | tf_op jit(solution)/shard_map/while
  95.2 5.2 %slice-start.1 = ((s8[5013504]{0:T(1024)(128)(4,1)}), s8[819200]{0:T(1024)(128)(4,1)S(1)}, s32[]{:S(2)}) async-start(s8[5013504]{0:T(1024)(128)(4,1)} %bitcast.181), calls=%async_computation.4 | async-start | bytes 1638400 | tf_op jit(solution)/shard_map/while
  106.7 5.2 %slice-start = ((s8[5013504]{0:T(1024)(128)(4,1)}), s8[4194304]{0:T(1024)(128)(4,1)S(1)}, s32[]{:S(2)}) async-start(s8[5013504]{0:T(1024)(128)(4,1)} %bitcast.181), calls=%async_computation.3 | async-start | bytes 8388608 | tf_op jit(solution)/shard_map/while
  106.7 5.2 %slice-start.1 = ((s8[5013504]{0:T(1024)(128)(4,1)}), s8[819200]{0:T(1024)(128)(4,1)S(1)}, s32[]{:S(2)}) async-start(s8[5013504]{0:T(1024)(128)(4,1)} %bitcast.181), calls=%async_computation.4 | async-start | bytes 1638400 | tf_op jit(solution)/shard_map/while
  118.2 5.2 %slice-start = ((s8[5013504]{0:T(1024)(128)(4,1)}), s8[4194304]{0:T(1024)(128)(4,1)S(1)}, s32[]{:S(2)}) async-start(s8[5013504]{0:T(1024)(128)(4,1)} %bitcast.181), calls=%async_computation.3 | async-start | bytes 8388608 | tf_op jit(solution)/shard_map/while
  118.2 5.2 %slice-start.1 = ((s8[5013504]{0:T(1024)(128)(4,1)}), s8[819200]{0:T(1024)(128)(4,1)S(1)}, s32[]{:S(2)}) async-start(s8[5013504]{0:T(1024)(128)(4,1)} %bitcast.181), calls=%async_computation.4 | async-start | bytes 1638400 | tf_op jit(solution)/shard_map/while
  129.7 5.2 %slice-start = ((s8[5013504]{0:T(1024)(128)(4,1)}), s8[4194304]{0:T(1024)(128)(4,1)S(1)}, s32[]{:S(2)}) async-start(s8[5013504]{0:T(1024)(128)(4,1)} %bitcast.181), calls=%async_computation.3 | async-start | bytes 8388608 | tf_op jit(solution)/shard_map/while
  129.7 5.2 %slice-start.1 = ((s8[5013504]{0:T(1024)(128)(4,1)}), s8[819200]{0:T(1024)(128)(4,1)S(1)}, s32[]{:S(2)}) async-start(s8[5013504]{0:T(1024)(128)(4,1)} %bitcast.181), calls=%async_computation.4 | async-start | bytes 1638400 | tf_op jit(solution)/shard_map/while
  141.2 5.2 %slice-start = ((s8[5013504]{0:T(1024)(128)(4,1)}), s8[4194304]{0:T(1024)(128)(4,1)S(1)}, s32[]{:S(2)}) async-start(s8[5013504]{0:T(1024)(128)(4,1)} %bitcast.181), calls=%async_computation.3 | async-start | bytes 8388608 | tf_op jit(solution)/shard_map/while
  141.2 5.2 %slice-start.1 = ((s8[5013504]{0:T(1024)(128)(4,1)}), s8[819200]{0:T(1024)(128)(4,1)S(1)}, s32[]{:S(2)}) async-start(s8[5013504]{0:T(1024)(128)(4,1)} %bitcast.181), calls=%async_computation.4 | async-start | bytes 1638400 | tf_op jit(solution)/shard_map/while
  153.6 3.9 %copy-start.1 = (f32[72,17408]{1,0:T(8,128)S(1)}, f32[72,17408]{1,0:T(8,128)}, u32[]{:S(2)}) copy-start(f32[72,17408]{1,0:T(8,128)} %get-tuple-element.103) | copy-start | bytes 15040516
  158.8 8.6 %collective-permute-start.1 = (bf16[5,136,128]{2,1,0:T(8,128)(2,1)S(1)}, bf16[5,136,128]{2,1,0:T(8,128)(2,1)S(1)}, u32[]{:S(2)}, u32[]{:S(2)}) collective-permute-start(bf16[5,136,128]{2,1,0:T(8,128)(2,1)S(1)} %bitcast.197), channel_id=1, source_target_pairs={{8,0},{16,8},{24,16},{9,1},{17,9},{25,17},{10,2},{18,10},{26,18},{... | collective-permute-start | bytes 522248 | tf_op jit(solution)/shard_map/ppermute | solution.py:21
  160.1 8.2 %collective-permute-start = (bf16[5,136,128]{2,1,0:T(8,128)(2,1)S(1)}, bf16[5,136,128]{2,1,0:T(8,128)(2,1)S(1)}, u32[]{:S(2)}, u32[]{:S(2)}) collective-permute-start(bf16[5,136,128]{2,1,0:T(8,128)(2,1)S(1)} %bitcast.193), channel_id=1, source_target_pairs={{0,8},{8,16},{16,24},{1,9},{9,17},{17,25},{2,10},{10,18},{18,26},{... | collective-permute-start | bytes 522248 | tf_op jit(solution)/shard_map/ppermute | solution.py:19
  168.8 6.6 %collective-permute-start.2 = (bf16[66,5,128]{2,1,0:T(8,128)(2,1)S(1)}, bf16[66,5,128]{2,1,0:T(8,128)(2,1)S(1)}, u32[]{:S(2)}, u32[]{:S(2)}) collective-permute-start(bf16[66,5,128]{2,1,0:T(8,128)(2,1)S(1)} %get-tuple-element.164), channel_id=1, source_target_pairs={{0,1},{1,2},{2,3},{3,4},{4,5},{5,6},{6,7},{7,0},{8,9},{9,10},{10,1... | collective-permute-start | bytes 253448 | tf_op jit(solution)/shard_map/ppermute | solution.py:19
  168.9 6.5 %collective-permute-start.3 = (bf16[66,5,128]{2,1,0:T(8,128)(2,1)S(1)}, bf16[66,5,128]{2,1,0:T(8,128)(2,1)S(1)}, u32[]{:S(2)}, u32[]{:S(2)}) collective-permute-start(bf16[66,5,128]{2,1,0:T(8,128)(2,1)S(1)} %get-tuple-element.165), channel_id=1, source_target_pairs={{1,0},{2,1},{3,2},{4,3},{5,4},{6,5},{7,6},{0,7},{9,8},{10,9},{11,1... | collective-permute-start | bytes 253448 | tf_op jit(solution)/shard_map/ppermute | solution.py:21
  197.9 2.5 copy-start.7
  (13 other events, 23.9 us)
Sparse Core Ops, SparseCore 0:
  198.0 130.6 all-reduce.1
where the time goes:
time: 338 us; the launch traced here: 337 us
  waiting for transfers between devices  132 us (39%)
  other arithmetic  64.7 us (19%)
  local copies, waits for them, and re-layouts  50.3 us (15%)
  matrix products  48.7 us (14%)
  starting transfers between devices  26.1 us (8%)
  between operations  15.1 us (4%)
    psum x1, waiting for transfers between devices, shards(): lax.psum(jnp.stack(weight_parts).reshape(3, 3, channels, channels), ('lat...  116 us
    mul x8, other arithmetic, accumulate(): lon_matrix[:, :, None] * rows_blk[:, None, :]  41.4 us
    dot_general x8, matrix products, accumulate(): lax.dot_general(lat_matrix, spread, (((0,), (0,)), ((), ())), preferred_e...  28.5 us
    while x48, local copies, waits for them, and re-layouts  17.9 us
    unnamed x31, local copies, waits for them, and re-layouts  13 us
    another operation x7, other arithmetic  12.8 us
    ppermute x4, starting transfers between devices, padded_2(): lax.ppermute(head, axis, [((i + 1) % count, i) for i in range(ends)])  11 us
    dot_general x9, matrix products, shards(): lax.dot_general(window, flat_grad, (((0,), (0,)), ((), ())), preferred_el...  10.5 us
  transfers between devices with their start and end apart: 11, of which 7 were waited for; matrix products, arithmetic and copies ran while one was open for 29% of the time, Pallas kernels for 0%

commit v1 on v0

v1 whole, which is shorter than its diff:
```python
import functools
import math

import jax
import jax.numpy as jnp
from jax import lax
from jax.experimental import pallas as pl
from jax.experimental.pallas import tpu as pltpu
from jax.sharding import PartitionSpec as P

rbf_scale = 1.5
taps = 8
before = 3
after = taps - 1 - before
geom_rows = 8
f32 = jnp.float32
bf16 = jnp.bfloat16


def pack_kernel(capacity, live_ref, rows_ref, owner_ref, lat_ref, lon_ref, pos_ref, out_ref):
    devices = out_ref.shape[0]
    row_total = rows_ref.shape[0]
    live = lax.broadcasted_iota(jnp.int32, (1, row_total), 1) < live_ref[0]
    owner = jnp.where(live, owner_ref[...], devices)
    match = lax.broadcasted_iota(jnp.int32, (devices, row_total), 0) == owner
    match = jnp.where(match, 1.0, 0.0)
    upper = lax.broadcasted_iota(jnp.int32, (row_total, row_total), 0) < lax.broadcasted_iota(
        jnp.int32, (row_total, row_total), 1
    )
    upper = jnp.where(upper, 1.0, 0.0).astype(bf16)
    earlier = jnp.dot(match.astype(bf16), upper, preferred_element_type=f32)
    rank = jnp.sum(earlier * match, axis=0, keepdims=True).astype(jnp.int32)
    slot = owner * capacity + rank
    geometry = jnp.concatenate(
        [
            pos_ref[...].astype(f32),
            lat_ref[...].astype(f32),
            lon_ref[...].astype(f32),
            jnp.where(live, 1.0, 0.0),
            jnp.zeros((geom_rows - 5, row_total), f32),
        ],
        axis=0,
    ).astype(bf16)
    group = max(1, min(devices, 256 // capacity))
    line = lax.broadcasted_iota(jnp.int32, (group * capacity, row_total), 0)
    for first in range(0, devices, group):
        hit = jnp.where(line == slot - first * capacity, 1.0, 0.0).astype(bf16)
        placed = jnp.dot(hit, rows_ref[...], preferred_element_type=f32).astype(bf16)
        info = lax.dot_general(
            geometry, hit, (((1,), (1,)), ((), ())), preferred_element_type=f32
        ).astype(bf16)
        for i in range(group):
            out_ref[first + i, 0:capacity, :] = placed[i * capacity : (i + 1) * capacity]
            out_ref[first + i, capacity : capacity + geom_rows, 0:capacity] = info[
                :, i * capacity : (i + 1) * capacity
            ]


def scatter_kernel(
    capacity,
    lanes,
    count_ref,
    lat_ref,
    lon_ref,
    fa_ref,
    fb_ref,
    msg_ref,
    own_ref,
    up_ref,
    down_ref,
    left_ref,
    right_ref,
    canvas,
    block,
):
    sources = msg_ref.shape[0]
    rows, cols = own_ref.shape[0], own_ref.shape[1]
    tall = canvas.shape[1]
    inv = 1.0 / (2.0 * rbf_scale * rbf_scale)

    def clear(i, _):
        for j in range(lanes):
            canvas[j, i] = jnp.zeros(canvas.shape[2:], f32)
        return 0

    lax.fori_loop(0, tall, clear, 0)
    line = lax.broadcasted_iota(jnp.int32, (taps, canvas.shape[3]), 0).astype(f32) - before
    level = [math.exp(-((a - before) ** 2 - before**2) * inv) for a in range(taps)]

    def source(src, _):
        block[...] = msg_ref[src, 0:capacity, :].astype(f32)

        def step(i, _):
            terms = []
            for j in range(lanes):
                s = i * lanes + j
                at = src * capacity + s
                fa = fa_ref[at]
                d = line - fb_ref[at]
                t = jnp.exp(-(d * d + (before + fa) * (before + fa)) * inv) * block[pl.ds(s, 1), :]
                g = jnp.exp(jnp.full(t.shape, 2.0 * inv, f32) * fa)
                terms.append((lat_ref[at], lon_ref[at], t, g))
            sums = []
            for j, (r, c, t, g) in enumerate(terms):
                for a in range(taps):
                    sums.append(canvas[j, r + a, pl.ds(c, taps), :] + t * level[a])
                    t = t * g
            for j, (r, c, _, _) in enumerate(terms):
                for a in range(taps):
                    canvas[j, r + a, pl.ds(c, taps), :] = sums[j * taps + a]
            return 0

        lax.fori_loop(0, (count_ref[src] + lanes - 1) // lanes, step, 0)
        return 0

    lax.fori_loop(0, sources, source, 0)
    up, down = before + 1, after + 1
    inset = before - 1

    def total(i):
        whole = canvas[0, i]
        for j in range(1, lanes):
            whole = whole + canvas[j, i]
        canvas[0, i] = whole

    def finish(i, _):
        total(i)
        return 0

    lax.fori_loop(0, tall, finish, 0)

    def emit(i, _):
        own_ref[i] = canvas[0, i + inset, inset : inset + cols, :].astype(bf16)
        left_ref[i] = canvas[0, i + inset, 0:up, :].astype(bf16)
        right_ref[i] = canvas[0, i + inset, inset + cols - 2 : inset + cols - 2 + down, :].astype(bf16)
        return 0

    lax.fori_loop(0, rows, emit, 0)
    for i in range(up):
        up_ref[i] = canvas[0, i].astype(bf16)
    for i in range(down):
        down_ref[i] = canvas[0, inset + rows - 2 + i].astype(bf16)


def conv_kernel(
    edge_ref,
    own_ref,
    up_ref,
    down_ref,
    left_ref,
    right_ref,
    ul_ref,
    ur_ref,
    dl_ref,
    dr_ref,
    feat_ref,
    weight_ref,
    ig_ref,
    wg_ref,
    grid,
    windows,
    turned,
    total,
):
    rows, cols = own_ref.shape[0], own_ref.shape[1]
    tile_lat, tile_lon, channels = feat_ref.shape
    up, down = before + 1, after + 1
    inset = before - 1

    def fill(i, _):
        grid[i, 0:cols, :] = own_ref[i].astype(f32)
        grid[i, 0:down, :] += right_ref[i].astype(f32)
        grid[i, cols - up : cols, :] += left_ref[i].astype(f32)
        return 0

    lax.fori_loop(0, rows, fill, 0)
    for i in range(up):
        at = rows - up + i
        grid[at, 0:cols, :] += up_ref[i, inset : inset + cols, :].astype(f32)
        grid[at, cols - up : cols, :] += ul_ref[i].astype(f32)
        grid[at, 0:down, :] += ur_ref[i].astype(f32)
    for i in range(down):
        grid[i, 0:cols, :] += down_ref[i, inset : inset + cols, :].astype(f32)
        grid[i, cols - up : cols, :] += dl_ref[i].astype(f32)
        grid[i, 0:down, :] += dr_ref[i].astype(f32)

    @pl.when(edge_ref[0] == 0)
    def _():
        grid[0] = jnp.zeros(grid.shape[1:], f32)

    @pl.when(edge_ref[0] == edge_ref[1] - 1)
    def _():
        grid[rows - 1] = jnp.zeros(grid.shape[1:], f32)

    def shift(i, _):
        for b in range(3):
            windows[pl.ds(pl.multiple_of(i * tile_lon, tile_lon), tile_lon), b * channels : (b + 1) * channels] = grid[
                i, 2 - b : 2 - b + tile_lon, :
            ].astype(bf16)
        return 0

    lax.fori_loop(0, rows, shift, 0)
    turned[:, 0 : 2 * tile_lon] = jnp.zeros((channels, 2 * tile_lon), bf16)
    turned[:, rows * tile_lon : (rows + 2) * tile_lon] = jnp.zeros((channels, 2 * tile_lon), bf16)

    def turn(p, _):
        turned[:, pl.ds(pl.multiple_of((p + 2) * tile_lon, tile_lon), tile_lon)] = feat_ref[p].T
        return 0

    lax.fori_loop(0, tile_lat, turn, 0)
    step = next(n for n in (11, 6, 3, 2, 1) if rows % n == 0)
    depth = step * tile_lon
    total[...] = jnp.zeros_like(total)

    def weigh(k, _):
        start = k * depth
        lhs = jnp.concatenate(
            [
                turned[:, pl.ds(pl.multiple_of(start + a * tile_lon, tile_lon), depth)]
                for a in range(3)
            ],
            axis=0,
        )
        rhs = windows[pl.ds(pl.multiple_of(start, tile_lon), depth), :]
        total[...] += jnp.dot(lhs, rhs, preferred_element_type=f32)
        return 0

    lax.fori_loop(0, rows // step, weigh, 0)
    for a in range(3):
        for b in range(3):
            wg_ref[a, b] = total[
                a * channels : (a + 1) * channels, b * channels : (b + 1) * channels
            ].astype(wg_ref.dtype)
    part = math.gcd(tile_lat, 8)

    def apply(k, _):
        acc = jnp.zeros((part * tile_lon, channels), f32)
        for a in range(3):
            start = pl.multiple_of((k * part + 2 - a) * tile_lon, tile_lon)
            acc = acc + jnp.dot(
                windows[pl.ds(start, part * tile_lon), :], weight_ref[a], preferred_element_type=f32
            )
        ig_ref[pl.ds(k * part, part)] = acc.reshape(part, tile_lon, channels).astype(bf16)
        return 0

    lax.fori_loop(0, tile_lat // part, apply, 0)


def shards(grad_rows, owner, lat_offset, lon_offset, position, live_count, features, conv_weight):
    lat_total = lax.axis_size("lat")
    lon_total = lax.axis_size("lon")
    device_total = lat_total * lon_total
    row_total, channels = grad_rows.shape
    tile_lat, tile_lon = features.shape[:2]
    capacity = max(2, 2 * row_total // device_total)
    smem = pl.BlockSpec(memory_space=pltpu.SMEM)
    vmem = pl.BlockSpec(memory_space=pltpu.VMEM)
    axes = ("lat", "lon")

    outgoing = pl.pallas_call(
        functools.partial(pack_kernel, capacity),
        out_shape=jax.ShapeDtypeStruct((device_total, capacity + geom_rows, channels), bf16),
        in_specs=[smem] + [vmem] * 5,
        out_specs=vmem,
        name="pack",
    )(
        live_count,
        grad_rows,
        owner.reshape(1, row_total),
        lat_offset.reshape(1, row_total),
        lon_offset.reshape(1, row_total),
        position.T,
    )
    incoming = lax.all_to_all(outgoing, axes, split_axis=0, concat_axis=0, tiled=True)
    info = incoming[:, capacity : capacity + 5, :capacity].astype(f32).transpose(1, 0, 2)
    counts = jnp.sum(info[4], axis=1).astype(jnp.int32)
    info = info.reshape(5, -1)

    rows, cols = tile_lat + 2, tile_lon + 2
    tall = tile_lat + taps - 1
    wide = -(-(tile_lon + taps - 1) // 8) * 8
    up, down = before + 1, after + 1
    lanes = math.gcd(capacity, 4)
    own, up_s, down_s, left_s, right_s = pl.pallas_call(
        functools.partial(scatter_kernel, capacity, lanes),
        out_shape=[
            jax.ShapeDtypeStruct((rows, cols, channels), bf16),
            jax.ShapeDtypeStruct((up, wide, channels), bf16),
            jax.ShapeDtypeStruct((down, wide, channels), bf16),
            jax.ShapeDtypeStruct((rows, up, channels), bf16),
            jax.ShapeDtypeStruct((rows, down, channels), bf16),
        ],
        in_specs=[smem] * 5 + [vmem],
        out_specs=[vmem] * 5,
        scratch_shapes=[
            pltpu.VMEM((lanes, tall, wide, channels), f32),
            pltpu.VMEM((capacity, channels), f32),
        ],
        compiler_params=pltpu.CompilerParams(vmem_limit_bytes=60 * 2**20),
        name="scatter",
    )(
        counts,
        info[2].astype(jnp.int32),
        info[3].astype(jnp.int32),
        info[0],
        info[1],
        incoming,
    )

    def move(x, da, db):
        pairs = []
        for i in range(lat_total):
            for j in range(lon_total):
                if 0 <= i + da < lat_total:
                    pairs.append(
                        (i * lon_total + j, (i + da) * lon_total + (j + db) % lon_total)
                    )
        return lax.ppermute(x, axes, pairs)

    inset = before - 1
    far = inset + cols - 2
    halo = [
        move(up_s, -1, 0),
        move(down_s, 1, 0),
        move(left_s, 0, -1),
        move(right_s, 0, 1),
        move(up_s[:, :up], -1, -1),
        move(up_s[:, far : far + down], -1, 1),
        move(down_s[:, :up], 1, -1),
        move(down_s[:, far : far + down], 1, 1),
    ]
    edge = jnp.stack([lax.axis_index("lat"), lat_total]).astype(jnp.int32)
    kernel_t = conv_weight.transpose(0, 1, 3, 2).reshape(3, 3 * channels, channels)
    input_grad, part = pl.pallas_call(
        conv_kernel,
        out_shape=[
            jax.ShapeDtypeStruct((tile_lat, tile_lon, channels), bf16),
            jax.ShapeDtypeStruct((3, 3, channels, channels), bf16),
        ],
        in_specs=[smem] + [vmem] * 11,
        out_specs=[vmem] * 2,
        scratch_shapes=[
            pltpu.VMEM((rows, -(-cols // 8) * 8, channels), f32),
            pltpu.VMEM((rows * tile_lon, 3 * channels), bf16),
            pltpu.VMEM((channels, (rows + 2) * tile_lon), bf16),
            pltpu.VMEM((3 * channels, 3 * channels), f32),
        ],
        compiler_params=pltpu.CompilerParams(vmem_limit_bytes=60 * 2**20),
        name="conv",
    )(edge, own, *halo, features, kernel_t)
    pieces = part.reshape(device_total, -1, channels)
    pieces = lax.all_to_all(pieces, axes, split_axis=0, concat_axis=0, tiled=True)
    mine = jnp.sum(pieces.astype(f32), axis=0).astype(bf16)
    spread = jnp.broadcast_to(mine[None], (device_total,) + mine.shape)
    spread = lax.all_to_all(spread, axes, split_axis=0, concat_axis=0, tiled=True)
    weight_grad = spread.reshape(3, 3, channels, channels).astype(f32)
    return input_grad, weight_grad


def solution(mesh):
    placed = (
        P(("lat", "lon"), None),
        P(("lat", "lon"), None),
        P(("lat", "lon")),
        P(("lat", "lon")),
        P(("lat", "lon"), None),
        P(("lat", "lon")),
        P("lat", "lon", None),
        P(),
    )
    return jax.shard_map(
        shards, mesh=mesh, in_specs=placed, out_specs=(P("lat", "lon", None), P()), check_vma=False
    )
```

time: 338 us -> 138 us (0.41)
  waiting for transfers between devices: 132 us -> 10.6 us
  other arithmetic: 64.7 us -> 1.68 us
  blocking collectives: 0 us -> 52.8 us
  matrix products: 48.7 us -> 0 us
  local copies, waits for them, and re-layouts: 50.3 us -> 9.04 us
  Pallas kernels: 0 us -> 38.8 us
  between operations: 15.1 us -> 1.49 us
    psum x1 -> x0, waiting for transfers between devices: 116 us -> none  [shards(): lax.psum(jnp.stack(weight_parts).reshape(3, 3, channels, channels), ('lat...]
    all_to_all x0 -> x3, blocking collectives: none -> 52.8 us  [the longest x1 25 us: shards(): lax.all_to_all(outgoing, axes, split_axis=0, concat_axis=0, tiled=True)]
    dot_general x26 -> x0, matrix products: 48.7 us -> none  [the longest x8 28.5 us: accumulate(): lax.dot_general(lat_matrix, spread, (((0,), (0,)), ((), ())), preferred_e...]
    mul x8 -> x0, other arithmetic: 41.4 us -> none  [accumulate(): lon_matrix[:, :, None] * rows_blk[:, None, :]]
    pallas_call x0 -> x3, Pallas kernels: none -> 38.8 us  [the longest x1 21.4 us: shards(): pl.pallas_call(conv_kernel, out_shape=[jax.ShapeDtypeStruct((tile_lat, ti...]
    while x48 -> x0, local copies, waits for them, and re-layouts: 17.9 us -> none
    another operation x8 -> x1, other arithmetic: 13.6 us -> 0.64 us  [shards(): edge = jnp.stack([lax.axis_index('lat'), lat_total]).astype(jnp.int32)]
    unnamed x31 -> x20, local copies, waits for them, and re-layouts: 13 us -> 0.73 us
  transfers between devices with their start and end apart: 11 -> 8, of which waited for: 7 -> 3; matrix products, arithmetic and copies ran while one was open for 29% -> 3% of each run, Pallas kernels for 0% -> 0%
where the time goes in v1:
time: 138 us
  blocking collectives  52.8 us (38%)
  Pallas kernels  38.8 us (28%)
  starting transfers between devices  23.7 us (17%)
  waiting for transfers between devices  10.6 us (8%)
  local copies, waits for them, and re-layouts  9.04 us (7%)
  other arithmetic  1.68 us (1%)
  between operations  1.49 us (1%)
    all_to_all x1, blocking collectives, shards(): lax.all_to_all(outgoing, axes, split_axis=0, concat_axis=0, tiled=True)  25 us
    ppermute x8, starting transfers between devices, move(): return lax.ppermute(x, axes, pairs)  23.7 us
    pallas_call x1, Pallas kernels, shards(): pl.pallas_call(conv_kernel, out_shape=[jax.ShapeDtypeStruct((tile_lat, ti...  21.4 us
    all_to_all x1, blocking collectives, shards(): lax.all_to_all(spread, axes, split_axis=0, concat_axis=0, tiled=True)  14.1 us
    all_to_all x1, blocking collectives, shards(): lax.all_to_all(pieces, axes, split_axis=0, concat_axis=0, tiled=True)  13.8 us
    pallas_call x1, Pallas kernels, shards(): pl.pallas_call(functools.partial(scatter_kernel, capacity, lanes), out_sh...  13.1 us
    ppermute x8, waiting for transfers between devices, move(): return lax.ppermute(x, axes, pairs)  10.6 us
    pallas_call x1, Pallas kernels, shards(): pl.pallas_call(functools.partial(pack_kernel, capacity), out_shape=jax.Sh...  4.29 us
  transfers between devices with their start and end apart: 8, of which 3 were waited for; matrix products, arithmetic and copies ran while one was open for 3% of the time, Pallas kernels for 0%

profile of v1, /device:TPU:0, one launch (start us, length us, event | category | flops | bytes accessed | tf_op | source)
XLA Modules:
  0.0 138.2 jit_solution(3057380870668707647)
XLA Ops:
  1.3 4.3 %pack.1 = bf16[32,72,128]{2,1,0:T(8,128)(2,1)} custom-call(s32[1]{0:T(128)S(6)} %copy.12.live_ref, bf16[1024,128]{1,0:T(8,128)(2,1)} %rows_ref.1, s32[1,1024]{1,0:T(1,128)} %bitcast.13, s32[1,1024]{1,0:T(1,128)} %bitcast.14, s32[1,1024]{1,0:T(1,128)} %bitcast.15, bf16[2,1024]{1,0:T(2,128)(2,1)} %bitcast.16), custom_call_target="tpu_custom_call" | custom-call | tf_op jit(solution)/shard_map/pack/pallas_call | solution.py:260
  5.6 25.0 %all_to_all.15.msg_ref = bf16[32,72,128]{2,1,0:T(8,128)(2,1)S(1)} all-to-all(bf16[32,72,128]{2,1,0:T(8,128)(2,1)} %pack.1), channel_id=1, replica_groups=mesh['lat'=4,'lon'=8] {'lat','lon'}, dimensions={0} | all-to-all | bytes 1179648 | tf_op jit(solution)/shard_map/all_to_all | solution.py:274
  30.6 0.1 fusion
  30.7 0.3 slice_reduce_fusion
  31.1 0.7 squeeze.10.fb_ref
  31.7 0.7 convert_element_type.26.lon_ref
  32.4 0.5 convert_element_type.22.count_ref
  32.9 0.7 convert_element_type.24.lat_ref
  33.6 0.7 squeeze.4.fa_ref
  34.2 13.1 %scatter.1 = (bf16[66,130,128]{2,1,0:T(8,128)(2,1)}, bf16[4,136,128]{2,1,0:T(8,128)(2,1)}, bf16[5,136,128]{2,1,0:T(8,128)(2,1)}, bf16[66,4,128]{2,1,0:T(4,128)(2,1)}, bf16[66,5,128]{2,1,0:T(8,128)(2,1)}) custom-call(s32[32]{0:T(128)} %convert_element_type.22.count_ref, s32[2048]{0:T(1024)} %convert_element_type.24.lat_ref, ...), custom_call_target="tpu_custom_call" | custom-call | tf_op jit(solution)/shard_map/scatter/pallas_call | solution.py:284
  47.3 9.9 %collective-permute-start.1 = (bf16[5,136,128]{2,1,0:T(8,128)(2,1)}, bf16[5,136,128]{2,1,0:T(8,128)(2,1)S(1)}, u32[]{:S(2)}, u32[]{:S(2)}) collective-permute-start(bf16[5,136,128]{2,1,0:T(8,128)(2,1)} %get-tuple-element.11), channel_id=1, source_target_pairs={{0,8},{1,9},{2,10},{3,11},{4,12},{5,13},{6,14},{7,15},{8,16},{9,17... | collective-permute-start | bytes 522248 | tf_op jit(solution)/shard_map/ppermute | solution.py:318
  57.3 1.3 collective-permute-start
  58.6 0.7 slice.42
  59.3 1.3 collective-permute-start.6
  60.5 0.7 slice.41
  61.2 1.3 collective-permute-start.5
  62.5 0.7 slice.40
  63.2 1.3 collective-permute-start.4
  64.5 0.7 slice.43
  65.2 5.7 %collective-permute-done.4.ul_ref = bf16[4,4,128]{2,1,0:T(4,128)(2,1)S(1)} collective-permute-done((bf16[4,4,128]{2,1,0:T(4,128)(2,1)S(1)}, bf16[4,4,128]{2,1,0:T(4,128)(2,1)S(1)}, u32[]{:S(2)}, u32[]{:S(2)}) %collective-permute-start.4) | collective-permute-done | bytes 4128 | tf_op jit(solution)/shard_map/ppermute | solution.py:318
  70.9 5.4 %collective-permute-start.7 = (bf16[5,5,128]{2,1,0:T(8,128)(2,1)S(1)}, bf16[5,5,128]{2,1,0:T(8,128)(2,1)S(1)}, u32[]{:S(2)}, u32[]{:S(2)}) collective-permute-start(bf16[5,5,128]{2,1,0:T(8,128)(2,1)S(1)} %slice.43), channel_id=1, source_target_pairs={{0,9},{1,10},{2,11},{3,12},{4,13},{5,14},{6,15},{7,8},{8,17},{9,18... | collective-permute-start | bytes 19208 | tf_op jit(solution)/shard_map/ppermute | solution.py:318
  76.4 3.2 %collective-permute-start.2 = (bf16[66,4,128]{2,1,0:T(4,128)(2,1)}, bf16[66,4,128]{2,1,0:T(4,128)(2,1)S(1)}, u32[]{:S(2)}, u32[]{:S(2)}) collective-permute-start(bf16[66,4,128]{2,1,0:T(4,128)(2,1)} %get-tuple-element.12), channel_id=1, source_target_pairs={{0,7},{1,0},{2,1},{3,2},{4,3},{5,4},{6,5},{7,6},{8,15},{9,8},{10,9... | collective-permute-start | bytes 202760 | tf_op jit(solution)/shard_map/ppermute | solution.py:318
  79.6 0.6 pad_add_fusion.edge_ref
  80.3 0.9 copy.11
  81.2 0.7 collective-permute-done.2.left_ref
  81.9 4.2 %collective-permute-done.3.right_ref = bf16[66,5,128]{2,1,0:T(8,128)(2,1)S(1)} collective-permute-done((bf16[66,5,128]{2,1,0:T(8,128)(2,1)}, bf16[66,5,128]{2,1,0:T(8,128)(2,1)S(1)}, u32[]{:S(2)}, u32[]{:S(2)}) %collective-permute-start.3) | collective-permute-done | bytes 84512 | tf_op jit(solution)/shard_map/ppermute | solution.py:318
  86.2 0.6 copy-done.4
  86.9 21.4 %conv.1 = (bf16[64,128,128]{2,1,0:T(8,128)(2,1)}, bf16[3,3,128,128]{3,2,1,0:T(8,128)(2,1)}) custom-call(s32[2]{0:T(128)} %pad_add_fusion.edge_ref, bf16[66,130,128]{2,1,0:T(8,128)(2,1)} %get-tuple-element.9.own_ref, bf16[4,136,128]{2,1,0:T(8,128)(2,1)} %copy-done.3, bf16[5,136,128]{2,1,0:T(8,128)(2,1)} %copy-done.2, bf16[66,4,128]{2,1,0:T(4,128)(2,1)} %copy-done.5, ...), custom_call_target="tpu_custom_call" | custom-call | tf_op jit(solution)/shard_map/conv/pallas_call | solution.py:334
  108.3 1.0 reshape.38
  109.3 13.8 %all_to_all.16 = bf16[32,36,128]{2,1,0:T(8,128)(2,1)S(1)} all-to-all(bf16[32,36,128]{2,1,0:T(8,128)(2,1)S(1)} %reshape.38), channel_id=1, replica_groups=mesh['lat'=4,'lon'=8] {'lat','lon'}, dimensions={0} | all-to-all | bytes 589824 | tf_op jit(solution)/shard_map/all_to_all | solution.py:352
  123.2 14.1 %all_to_all.17 = bf16[32,36,128]{2,1,0:T(8,128)(2,1)S(1)} all-to-all(bf16[32,36,128]{2,1,0:T(8,128)(2,1)S(1)} %broadcast_in_dim.2), channel_id=1, replica_groups=mesh['lat'=4,'lon'=8] {'lat','lon'}, dimensions={0} | all-to-all | bytes 589824 | tf_op jit(solution)/shard_map/all_to_all | solution.py:355
  137.3 0.9 reshape.39
  (28 shorter events, 0.3 us)
Async XLA Ops:
  0.6 79.7 %copy-start.1 = (bf16[3,3,128,128]{3,2,1,0:T(8,128)(2,1)S(1)}, bf16[3,3,128,128]{3,2,1,0:T(8,128)(2,1)}, u32[]{:S(2)}) copy-start(bf16[3,3,128,128]{3,2,1,0:T(8,128)(2,1)} %param.15) | copy-start | bytes 884740
  30.6 3.6 %copy-start = (bf16[32,72,128]{2,1,0:T(8,128)(2,1)}, bf16[32,72,128]{2,1,0:T(8,128)(2,1)S(1)}, u32[]{:S(2)}) copy-start(bf16[32,72,128]{2,1,0:T(8,128)(2,1)S(1)} %all_to_all.15.msg_ref) | copy-start | bytes 1769476
  47.3 38.8 %collective-permute-start.1 = (bf16[5,136,128]{2,1,0:T(8,128)(2,1)}, bf16[5,136,128]{2,1,0:T(8,128)(2,1)S(1)}, u32[]{:S(2)}, u32[]{:S(2)}) collective-permute-start(bf16[5,136,128]{2,1,0:T(8,128)(2,1)} %get-tuple-element.11), channel_id=1, source_target_pairs={{0,8},{1,9},{2,10},{3,11},{4,12},{5,13},{6,14},{7,15},{8,16},{9,17... | collective-permute-start | bytes 522248 | tf_op jit(solution)/shard_map/ppermute | solution.py:318
  57.3 28.8 %collective-permute-start = (bf16[4,136,128]{2,1,0:T(8,128)(2,1)}, bf16[4,136,128]{2,1,0:T(8,128)(2,1)S(1)}, u32[]{:S(2)}, u32[]{:S(2)}) collective-permute-start(bf16[4,136,128]{2,1,0:T(8,128)(2,1)} %get-tuple-element.10), channel_id=1, source_target_pairs={{8,0},{9,1},{10,2},{11,3},{12,4},{13,5},{14,6},{15,7},{16,8},{17,9... | collective-permute-start | bytes 417800 | tf_op jit(solution)/shard_map/ppermute | solution.py:318
  59.3 17.1 %collective-permute-start.6 = (bf16[5,4,128]{2,1,0:T(4,128)(2,1)S(1)}, bf16[5,4,128]{2,1,0:T(4,128)(2,1)S(1)}, u32[]{:S(2)}, u32[]{:S(2)}) collective-permute-start(bf16[5,4,128]{2,1,0:T(4,128)(2,1)S(1)} %slice.42), channel_id=1, source_target_pairs={{0,15},{1,8},{2,9},{3,10},{4,11},{5,12},{6,13},{7,14},{8,23},{9,16... | collective-permute-start | bytes 15368 | tf_op jit(solution)/shard_map/ppermute | solution.py:318
  61.2 18.4 %collective-permute-start.5 = (bf16[4,5,128]{2,1,0:T(8,128)(2,1)S(1)}, bf16[4,5,128]{2,1,0:T(8,128)(2,1)S(1)}, u32[]{:S(2)}, u32[]{:S(2)}) collective-permute-start(bf16[4,5,128]{2,1,0:T(8,128)(2,1)S(1)} %slice.41), channel_id=1, source_target_pairs={{8,1},{9,2},{10,3},{11,4},{12,5},{13,6},{14,7},{15,0},{16,9},{17,1... | collective-permute-start | bytes 15368 | tf_op jit(solution)/shard_map/ppermute | solution.py:318
  63.2 7.7 %collective-permute-start.4 = (bf16[4,4,128]{2,1,0:T(4,128)(2,1)S(1)}, bf16[4,4,128]{2,1,0:T(4,128)(2,1)S(1)}, u32[]{:S(2)}, u32[]{:S(2)}) collective-permute-start(bf16[4,4,128]{2,1,0:T(4,128)(2,1)S(1)} %slice.40), channel_id=1, source_target_pairs={{8,7},{9,0},{10,1},{11,2},{12,3},{13,4},{14,5},{15,6},{16,15},{17,... | collective-permute-start | bytes 12296 | tf_op jit(solution)/shard_map/ppermute | solution.py:318
  70.9 15.2 %copy-start.9 = (bf16[4,4,128]{2,1,0:T(4,128)(2,1)}, bf16[4,4,128]{2,1,0:T(4,128)(2,1)S(1)}, u32[]{:S(2)}) copy-start(bf16[4,4,128]{2,1,0:T(4,128)(2,1)S(1)} %collective-permute-done.4.ul_ref) | copy-start | bytes 12292
  70.9 10.2 %collective-permute-start.7 = (bf16[5,5,128]{2,1,0:T(8,128)(2,1)S(1)}, bf16[5,5,128]{2,1,0:T(8,128)(2,1)S(1)}, u32[]{:S(2)}, u32[]{:S(2)}) collective-permute-start(bf16[5,5,128]{2,1,0:T(8,128)(2,1)S(1)} %slice.43), channel_id=1, source_target_pairs={{0,9},{1,10},{2,11},{3,12},{4,13},{5,14},{6,15},{7,8},{8,17},{9,18... | collective-permute-start | bytes 19208 | tf_op jit(solution)/shard_map/ppermute | solution.py:318
  76.4 9.7 %copy-start.8 = (bf16[5,4,128]{2,1,0:T(4,128)(2,1)}, bf16[5,4,128]{2,1,0:T(4,128)(2,1)S(1)}, u32[]{:S(2)}) copy-start(bf16[5,4,128]{2,1,0:T(4,128)(2,1)S(1)} %collective-permute-done.6.dl_ref) | copy-start | bytes 15364
  76.4 5.5 %collective-permute-start.2 = (bf16[66,4,128]{2,1,0:T(4,128)(2,1)}, bf16[66,4,128]{2,1,0:T(4,128)(2,1)S(1)}, u32[]{:S(2)}, u32[]{:S(2)}) collective-permute-start(bf16[66,4,128]{2,1,0:T(4,128)(2,1)} %get-tuple-element.12), channel_id=1, source_target_pairs={{0,7},{1,0},{2,1},{3,2},{4,3},{5,4},{6,5},{7,6},{8,15},{9,8},{10,9... | collective-permute-start | bytes 202760 | tf_op jit(solution)/shard_map/ppermute | solution.py:318
  79.6 6.5 %copy-start.7 = (bf16[4,5,128]{2,1,0:T(8,128)(2,1)}, bf16[4,5,128]{2,1,0:T(8,128)(2,1)S(1)}, u32[]{:S(2)}) copy-start(bf16[4,5,128]{2,1,0:T(8,128)(2,1)S(1)} %collective-permute-done.5.ur_ref) | copy-start | bytes 15364
  79.6 6.4 %collective-permute-start.3 = (bf16[66,5,128]{2,1,0:T(8,128)(2,1)}, bf16[66,5,128]{2,1,0:T(8,128)(2,1)S(1)}, u32[]{:S(2)}, u32[]{:S(2)}) collective-permute-start(bf16[66,5,128]{2,1,0:T(8,128)(2,1)} %get-tuple-element.13), channel_id=1, source_target_pairs={{0,1},{1,2},{2,3},{3,4},{4,5},{5,6},{6,7},{7,0},{8,9},{9,10},{10,1... | collective-permute-start | bytes 253448 | tf_op jit(solution)/shard_map/ppermute | solution.py:318
  81.2 5.0 %copy-start.6 = (bf16[5,5,128]{2,1,0:T(8,128)(2,1)}, bf16[5,5,128]{2,1,0:T(8,128)(2,1)S(1)}, u32[]{:S(2)}) copy-start(bf16[5,5,128]{2,1,0:T(8,128)(2,1)S(1)} %collective-permute-done.7.dr_ref) | copy-start | bytes 19204
  81.9 4.3 %copy-start.5 = (bf16[66,4,128]{2,1,0:T(4,128)(2,1)}, bf16[66,4,128]{2,1,0:T(4,128)(2,1)S(1)}, u32[]{:S(2)}) copy-start(bf16[66,4,128]{2,1,0:T(4,128)(2,1)S(1)} %collective-permute-done.2.left_ref) | copy-start | bytes 202756
  86.1 0.7 copy-start.4
  86.1 0.7 copy-start.3
  86.1 0.8 copy-start.2

commit v2 on v1

--- a/solution.py
+++ b/solution.py
@@ -70,6 +70,10 @@
     down_ref,
     left_ref,
     right_ref,
+    ul_ref,
+    ur_ref,
+    dl_ref,
+    dr_ref,
     canvas,
     block,
 ):
@@ -136,81 +140,123 @@
         return 0
 
     lax.fori_loop(0, rows, emit, 0)
-    for i in range(up):
-        up_ref[i] = canvas[0, i].astype(bf16)
-    for i in range(down):
-        down_ref[i] = canvas[0, inset + rows - 2 + i].astype(bf16)
+    spans = ((0, up), (inset, cols), (inset + cols - 2, down))
+    for count, first, refs in (
+        (up, 0, (ul_ref, up_ref, ur_ref)),
+        (down, inset + rows - 2, (dl_ref, down_ref, dr_ref)),
+    ):
+        for i in range(count):
+            for (start, width), ref in zip(spans, refs):
+                ref[i] = canvas[0, first + i, start : start + width, :].astype(bf16)
 
 
 def conv_kernel(
-    edge_ref,
+    lat_total,
+    lon_total,
     own_ref,
-    up_ref,
-    down_ref,
-    left_ref,
-    right_ref,
-    ul_ref,
-    ur_ref,
-    dl_ref,
-    dr_ref,
-    feat_ref,
-    weight_ref,
-    ig_ref,
-    wg_ref,
-    grid,
-    windows,
-    turned,
-    total,
+    *refs,
 ):
+    strips, (feat_ref, weight_ref, ig_ref, wg_ref) = refs[:8], refs[8:12]
+    landed = refs[12:20]
+    (grid, windows, turned, total, flat, pieces, parts, mine, gathered) = refs[20:29]
+    halo_send, halo_recv, part_send, part_recv, all_send, all_recv = refs[29:]
     rows, cols = own_ref.shape[0], own_ref.shape[1]
     tile_lat, tile_lon, channels = feat_ref.shape
     up, down = before + 1, after + 1
-    inset = before - 1
+    devices = lat_total * lon_total
+    lat, lon = lax.axis_index("lat"), lax.axis_index("lon")
+    me = lat * lon_total + lon
+
+    def place(peer):
+        return (peer // lon_total, peer % lon_total)
+
+    barrier = pltpu.get_barrier_semaphore()
+
+    def greet(k, _):
+        pl.semaphore_signal(
+            barrier, inc=1, device_id=place((me + k) % devices), device_id_type=pl.DeviceIdType.MESH
+        )
+        return 0
+
+    lax.fori_loop(1, devices, greet, 0)
 
     def fill(i, _):
         grid[i, 0:cols, :] = own_ref[i].astype(f32)
-        grid[i, 0:down, :] += right_ref[i].astype(f32)
-        grid[i, cols - up : cols, :] += left_ref[i].astype(f32)
         return 0
 
     lax.fori_loop(0, rows, fill, 0)
-    for i in range(up):
-        at = rows - up + i
-        grid[at, 0:cols, :] += up_ref[i, inset : inset + cols, :].astype(f32)
-        grid[at, cols - up : cols, :] += ul_ref[i].astype(f32)
-        grid[at, 0:down, :] += ur_ref[i].astype(f32)
-    for i in range(down):
-        grid[i, 0:cols, :] += down_ref[i, inset : inset + cols, :].astype(f32)
-        grid[i, cols - up : cols, :] += dl_ref[i].astype(f32)
-        grid[i, 0:down, :] += dr_ref[i].astype(f32)
-
-    @pl.when(edge_ref[0] == 0)
+    pl.semaphore_wait(barrier, devices - 1)
+
+    ways = ((-1, 0), (1, 0), (0, -1), (0, 1), (-1, -1), (-1, 1), (1, -1), (1, 1))
+    halos = []
+    for w, (da, db) in enumerate(ways):
+        copy = pltpu.make_async_remote_copy(
+            src_ref=strips[w],
+            dst_ref=landed[w],
+            send_sem=halo_send.at[w],
+            recv_sem=halo_recv.at[w],
+            device_id=((lat + da + lat_total) % lat_total, (lon + db + lon_total) % lon_total),
+            device_id_type=pl.DeviceIdType.MESH,
+        )
+        sends = (lat + da >= 0) & (lat + da < lat_total)
+        takes = (lat - da >= 0) & (lat - da < lat_total)
+        halos.append((copy, sends, takes))
+
+    def when(da, cond, fn):
+        if da == 0:
+            fn()
+        else:
+            pl.when(cond)(fn)
+
+    for (copy, sends, _), (da, _) in zip(halos, ways):
+        when(da, sends, copy.start)
+
+    turned[:, 0 : 2 * tile_lon] = jnp.zeros((channels, 2 * tile_lon), bf16)
+    turned[:, rows * tile_lon : (rows + 2) * tile_lon] = jnp.zeros((channels, 2 * tile_lon), bf16)
+
+    def turn(p, _):
+        turned[:, pl.ds(pl.multiple_of((p + 2) * tile_lon, tile_lon), tile_lon)] = feat_ref[p].T
+        return 0
+
+    lax.fori_loop(0, tile_lat, turn, 0)
+    total[...] = jnp.zeros_like(total)
+
+    for (copy, _, takes), (da, db), ref in zip(halos, ways, landed):
+
+        def take(copy=copy, da=da, db=db, ref=ref):
+            copy.wait_recv()
+            high = {-1: rows - up, 0: 0, 1: 0}[da]
+            count = {-1: up, 0: rows, 1: down}[da]
+            left = {-1: cols - up, 0: 0, 1: 0}[db]
+            width = {-1: up, 0: cols, 1: down}[db]
+
+            def add(i, _):
+                grid[high + i, left : left + width, :] += ref[i].astype(f32)
+                return 0
+
+            lax.fori_loop(0, count, add, 0)
+
+        when(da, takes, take)
+
+    @pl.when(lat == 0)
     def _():
         grid[0] = jnp.zeros(grid.shape[1:], f32)
 
-    @pl.when(edge_ref[0] == edge_ref[1] - 1)
+    @pl.when(lat == lat_total - 1)
     def _():
         grid[rows - 1] = jnp.zeros(grid.shape[1:], f32)
 
     def shift(i, _):
+        at = pl.ds(pl.multiple_of(i * tile_lon, tile_lon), tile_lon)
         for b in range(3):
-            windows[pl.ds(pl.multiple_of(i * tile_lon, tile_lon), tile_lon), b * channels : (b + 1) * channels] = grid[
+            windows[at, b * channels : (b + 1) * channels] = grid[
                 i, 2 - b : 2 - b + tile_lon, :
             ].astype(bf16)
         return 0
 
     lax.fori_loop(0, rows, shift, 0)
-    turned[:, 0 : 2 * tile_lon] = jnp.zeros((channels, 2 * tile_lon), bf16)
-    turned[:, rows * tile_lon : (rows + 2) * tile_lon] = jnp.zeros((channels, 2 * tile_lon), bf16)
-
-    def turn(p, _):
-        turned[:, pl.ds(pl.multiple_of((p + 2) * tile_lon, tile_lon), tile_lon)] = feat_ref[p].T
-        return 0
-
-    lax.fori_loop(0, tile_lat, turn, 0)
     step = next(n for n in (11, 6, 3, 2, 1) if rows % n == 0)
     depth = step * tile_lon
-    total[...] = jnp.zeros_like(total)
 
     def weigh(k, _):
         start = k * depth
@@ -228,10 +274,20 @@
     lax.fori_loop(0, rows // step, weigh, 0)
     for a in range(3):
         for b in range(3):
-            wg_ref[a, b] = total[
+            at = (a * 3 + b) * channels
+            flat[at : at + channels, :] = total[
                 a * channels : (a + 1) * channels, b * channels : (b + 1) * channels
-            ].astype(wg_ref.dtype)
+            ]
+    share = pieces.shape[1]
+
+    def cut(d, _):
+        pieces[d] = flat[pl.ds(d * share, share), :].astype(bf16)
+        return 0
+
+    lax.fori_loop(0, devices, cut, 0)
     part = math.gcd(tile_lat, 8)
+    strides = tile_lat // part
+    half = strides // 2
 
     def apply(k, _):
         acc = jnp.zeros((part * tile_lon, channels), f32)
@@ -243,7 +299,58 @@
         ig_ref[pl.ds(k * part, part)] = acc.reshape(part, tile_lon, channels).astype(bf16)
         return 0
 
-    lax.fori_loop(0, tile_lat // part, apply, 0)
+    def scattered(peer, slot):
+        return pltpu.make_async_remote_copy(
+            src_ref=pieces.at[peer],
+            dst_ref=parts.at[slot],
+            send_sem=part_send.at[peer],
+            recv_sem=part_recv.at[slot],
+            device_id=place(peer),
+            device_id_type=pl.DeviceIdType.MESH,
+        )
+
+    def shared(peer, slot):
+        return pltpu.make_async_remote_copy(
+            src_ref=mine,
+            dst_ref=gathered.at[slot],
+            send_sem=all_send.at[peer],
+            recv_sem=all_recv.at[slot],
+            device_id=place(peer),
+            device_id_type=pl.DeviceIdType.MESH,
+        )
+
+    def each(fn):
+        def body(k, _):
+            fn((me + k) % devices)
+            return 0
+
+        lax.fori_loop(1, devices, body, 0)
+
+    each(lambda peer: scattered(peer, me).start())
+    lax.fori_loop(0, half, apply, 0)
+    each(lambda peer: scattered(peer, peer).wait_recv())
+    parts[me] = pieces[me]
+
+    def gather_sum(d, acc):
+        return acc + parts[d].astype(f32)
+
+    mine[...] = lax.fori_loop(
+        0, devices, gather_sum, jnp.zeros((share, channels), f32)
+    ).astype(bf16)
+    each(lambda peer: shared(peer, me).start())
+    lax.fori_loop(half, strides, apply, 0)
+    each(lambda peer: shared(peer, peer).wait_recv())
+    gathered[me] = mine[...]
+
+    def spill(d, _):
+        wg_ref[pl.ds(d * share, share), :] = gathered[d].astype(f32)
+        return 0
+
+    lax.fori_loop(0, devices, spill, 0)
+    for (copy, sends, _), (da, _) in zip(halos, ways):
+        when(da, sends, copy.wait_send)
+    each(lambda peer: scattered(peer, me).wait_send())
+    each(lambda peer: shared(peer, me).wait_send())
 
 
 def shards(grad_rows, owner, lat_offset, lon_offset, position, live_count, features, conv_weight):
@@ -281,17 +388,24 @@
     wide = -(-(tile_lon + taps - 1) // 8) * 8
     up, down = before + 1, after + 1
     lanes = math.gcd(capacity, 4)
-    own, up_s, down_s, left_s, right_s = pl.pallas_call(
+    strip_shapes = [
+        (up, cols),
+        (down, cols),
+        (rows, up),
+        (rows, down),
+        (up, up),
+        (up, down),
+        (down, up),
+        (down, down),
+    ]
+    own, *strips = pl.pallas_call(
         functools.partial(scatter_kernel, capacity, lanes),
         out_shape=[
-            jax.ShapeDtypeStruct((rows, cols, channels), bf16),
-            jax.ShapeDtypeStruct((up, wide, channels), bf16),
-            jax.ShapeDtypeStruct((down, wide, channels), bf16),
-            jax.ShapeDtypeStruct((rows, up, channels), bf16),
-            jax.ShapeDtypeStruct((rows, down, channels), bf16),
+            jax.ShapeDtypeStruct(shape + (channels,), bf16)
+            for shape in [(rows, cols)] + strip_shapes
         ],
         in_specs=[smem] * 5 + [vmem],
-        out_specs=[vmem] * 5,
+        out_specs=[vmem] * 9,
         scratch_shapes=[
             pltpu.VMEM((lanes, tall, wide, channels), f32),
             pltpu.VMEM((capacity, channels), f32),
@@ -306,55 +420,42 @@
         info[1],
         incoming,
     )
-
-    def move(x, da, db):
-        pairs = []
-        for i in range(lat_total):
-            for j in range(lon_total):
-                if 0 <= i + da < lat_total:
-                    pairs.append(
-                        (i * lon_total + j, (i + da) * lon_total + (j + db) % lon_total)
-                    )
-        return lax.ppermute(x, axes, pairs)
-
-    inset = before - 1
-    far = inset + cols - 2
-    halo = [
-        move(up_s, -1, 0),
-        move(down_s, 1, 0),
-        move(left_s, 0, -1),
-        move(right_s, 0, 1),
-        move(up_s[:, :up], -1, -1),
-        move(up_s[:, far : far + down], -1, 1),
-        move(down_s[:, :up], 1, -1),
-        move(down_s[:, far : far + down], 1, 1),
-    ]
-    edge = jnp.stack([lax.axis_index("lat"), lat_total]).astype(jnp.int32)
     kernel_t = conv_weight.transpose(0, 1, 3, 2).reshape(3, 3 * channels, channels)
-    input_grad, part = pl.pallas_call(
-        conv_kernel,
+    flat_rows = 9 * channels
+    share = flat_rows // device_total
+    ring = pltpu.VMEM((device_total, share, channels), bf16)
+    input_grad, weight_grad = pl.pallas_call(
+        functools.partial(conv_kernel, lat_total, lon_total),
         out_shape=[
             jax.ShapeDtypeStruct((tile_lat, tile_lon, channels), bf16),
-            jax.ShapeDtypeStruct((3, 3, channels, channels), bf16),
+            jax.ShapeDtypeStruct((flat_rows, channels), f32),
         ],
-        in_specs=[smem] + [vmem] * 11,
+        in_specs=[vmem] * 11,
         out_specs=[vmem] * 2,
-        scratch_shapes=[
+        scratch_shapes=[pltpu.VMEM(shape + (channels,), bf16) for shape in strip_shapes]
+        + [
             pltpu.VMEM((rows, -(-cols // 8) * 8, channels), f32),
             pltpu.VMEM((rows * tile_lon, 3 * channels), bf16),
             pltpu.VMEM((channels, (rows + 2) * tile_lon), bf16),
             pltpu.VMEM((3 * channels, 3 * channels), f32),
+            pltpu.VMEM((flat_rows, channels), f32),
+            ring,
+            ring,
+            pltpu.VMEM((share, channels), bf16),
+            ring,
+            pltpu.SemaphoreType.DMA((8,)),
+            pltpu.SemaphoreType.DMA((8,)),
+            pltpu.SemaphoreType.DMA((device_total,)),
+            pltpu.SemaphoreType.DMA((device_total,)),
+            pltpu.SemaphoreType.DMA((device_total,)),
+            pltpu.SemaphoreType.DMA((device_total,)),
         ],
-        compiler_params=pltpu.CompilerParams(vmem_limit_bytes=60 * 2**20),
+        compiler_params=pltpu.CompilerParams(
+            vmem_limit_bytes=60 * 2**20, collective_id=0, has_side_effects=True
+        ),
         name="conv",
-    )(edge, own, *halo, features, kernel_t)
-    pieces = part.reshape(device_total, -1, channels)
-    pieces = lax.all_to_all(pieces, axes, split_axis=0, concat_axis=0, tiled=True)
-    mine = jnp.sum(pieces.astype(f32), axis=0).astype(bf16)
-    spread = jnp.broadcast_to(mine[None], (device_total,) + mine.shape)
-    spread = lax.all_to_all(spread, axes, split_axis=0, concat_axis=0, tiled=True)
-    weight_grad = spread.reshape(3, 3, channels, channels).astype(f32)
-    return input_grad, weight_grad
+    )(own, *strips, features, kernel_t)
+    return input_grad, weight_grad.reshape(3, 3, channels, channels)
 
 
 def solution(mesh):

time: 138 us -> 102 us (0.74)
  blocking collectives: 52.8 us -> 0 us
  Pallas kernels: 38.8 us -> 67.5 us
  starting transfers between devices: 23.7 us -> 7.33 us
  waiting for transfers between devices: 10.6 us -> 16.7 us
  local copies, waits for them, and re-layouts: 9.04 us -> 7.6 us
    all_to_all x3 -> x0, blocking collectives: 52.8 us -> none  [the longest x1 25 us: shards(): lax.all_to_all(outgoing, axes, split_axis=0, concat_axis=0, tiled=True)]
    pallas_call x1, Pallas kernels: 21.4 us -> 45.5 us  [shards(): pl.pallas_call(functools.partial(conv_kernel, lat_total, lon_total), out_...]
    ppermute x8 -> x0, starting transfers between devices: 23.7 us -> none  [move(): return lax.ppermute(x, axes, pairs)]
    all_to_all x0 -> x1, waiting for transfers between devices: none -> 16.7 us  [shards(): lax.all_to_all(outgoing, axes, split_axis=0, concat_axis=0, tiled=True)]
    ppermute x8 -> x0, waiting for transfers between devices: 10.6 us -> none  [move(): return lax.ppermute(x, axes, pairs)]
    all_to_all x0 -> x1, starting transfers between devices: none -> 7.33 us  [shards(): lax.all_to_all(outgoing, axes, split_axis=0, concat_axis=0, tiled=True)]
    pallas_call x1, Pallas kernels: 13.1 us -> 17.7 us  [shards(): pl.pallas_call(functools.partial(scatter_kernel, capacity, lanes), out_sh...]
    unnamed x20 -> x8, local copies, waits for them, and re-layouts: 0.73 us -> 4.05 us
  transfers between devices with their start and end apart: 8 -> 1, of which waited for: 3 -> 1; matrix products, arithmetic and copies ran while one was open for 3% -> 1% of each run, Pallas kernels for 0% -> 0%
where the time goes in v2:
time: 102 us
  Pallas kernels  67.5 us (66%)
  waiting for transfers between devices  16.7 us (16%)
  local copies, waits for them, and re-layouts  7.6 us (7%)
  starting transfers between devices  7.33 us (7%)
  between operations  1.38 us (1%)
    pallas_call x1, Pallas kernels, shards(): pl.pallas_call(functools.partial(conv_kernel, lat_total, lon_total), out_...  45.5 us
    pallas_call x1, Pallas kernels, shards(): pl.pallas_call(functools.partial(scatter_kernel, capacity, lanes), out_sh...  17.7 us
    all_to_all x1, waiting for transfers between devices, shards(): lax.all_to_all(outgoing, axes, split_axis=0, concat_axis=0, tiled=True)  16.7 us
    all_to_all x1, starting transfers between devices, shards(): lax.all_to_all(outgoing, axes, split_axis=0, concat_axis=0, tiled=True)  7.33 us
    pallas_call x1, Pallas kernels, shards(): pl.pallas_call(functools.partial(pack_kernel, capacity), out_shape=jax.Sh...  4.29 us
    unnamed x8, local copies, waits for them, and re-layouts  4.05 us
  transfers between devices with their start and end apart: 1, of which 1 were waited for; matrix products, arithmetic and copies ran while one was open for 1% of the time, Pallas kernels for 0%

profile of v2, /device:TPU:0, one launch (start us, length us, event | category | flops | bytes accessed | tf_op | source)
XLA Modules:
  0.0 101.5 jit_solution(10779969005199148195)
XLA Ops:
  0.6 0.0 copy-start.2
  1.3 4.3 %pack.1 = bf16[32,72,128]{2,1,0:T(8,128)(2,1)} custom-call(s32[1]{0:T(128)S(6)} %copy.13.live_ref, bf16[1024,128]{1,0:T(8,128)(2,1)} %rows_ref.1, s32[1,1024]{1,0:T(1,128)} %bitcast.12, s32[1,1024]{1,0:T(1,128)} %bitcast.13, s32[1,1024]{1,0:T(1,128)} %bitcast.14, bf16[2,1024]{1,0:T(2,128)(2,1)} %bitcast.15), custom_call_target="tpu_custom_call" | custom-call | tf_op jit(solution)/shard_map/pack/pallas_call | solution.py:367
  5.6 7.3 %all-to-all-start = ((bf16[32,72,128]{2,1,0:T(8,128)(2,1)}), bf16[32,72,128]{2,1,0:T(8,128)(2,1)S(1)}, u32[]{:S(2)}, u32[]{:S(2)}) async-start(bf16[32,72,128]{2,1,0:T(8,128)(2,1)} %pack.1), calls=%async_computation | async-start | bytes 1179648 | tf_op jit(solution)/shard_map/all_to_all | solution.py:381
  13.0 0.0 copy-done.2
  13.0 0.9 copy.10
  13.9 16.7 %all-to-all-done.msg_ref = bf16[32,72,128]{2,1,0:T(8,128)(2,1)S(1)} async-done(((bf16[32,72,128]{2,1,0:T(8,128)(2,1)}), bf16[32,72,128]{2,1,0:T(8,128)(2,1)S(1)}, u32[]{:S(2)}, u32[]{:S(2)}) %all-to-all-start) | async-done | bytes 589856 | tf_op jit(solution)/shard_map/all_to_all | solution.py:381
  30.6 0.0 copy-start
  30.6 0.1 fusion
  30.7 0.3 slice_reduce_fusion
  31.1 0.7 squeeze.10.fb_ref
  31.7 0.7 convert_element_type.18.lon_ref
  32.4 0.5 convert_element_type.14.count_ref
  32.9 0.7 convert_element_type.16.lat_ref
  33.6 0.7 squeeze.4.fa_ref
  34.3 0.0 copy-done
  34.3 17.7 %scatter.1 = (bf16[66,130,128]{2,1,0:T(8,128)(2,1)}, bf16[4,130,128]{2,1,0:T(8,128)(2,1)}, bf16[5,130,128]{2,1,0:T(8,128)(2,1)}, bf16[66,4,128]{2,1,0:T(4,128)(2...) custom-call(s32[32]{0:T(128)} %convert_element_type.14.count_ref, ...), custom_call_target="tpu_custom_call" | custom-call | tf_op jit(solution)/shard_map/scatter/pallas_call | solution.py:401
  52.0 45.5 %conv.1 = (bf16[64,128,128]{2,1,0:T(8,128)(2,1)}, f32[1152,128]{1,0:T(8,128)}) custom-call(bf16[66,130,128]{2,1,0:T(8,128)(2,1)} %get-tuple-element.13.own_ref, bf16[4,130,128]{2,1,0:T(8,128)(2,1)} %get-tuple-element.14.refs_0_, bf16[5,130,128]{2,1,0:T(8,128)(2,1)} %get-tuple-element.15.refs_1_, bf16[66,4,128]{2,1,0:T(4,128)(2,1)} %get-tuple-element.16.refs_2_, ...), custom_call_target="tpu_custom_call" | custom-call | tf_op jit(solution)/shard_map/conv/pallas_call | solution.py:427
  97.5 0.0 copy-start.1
  97.5 3.2 %copy.14 = bf16[64,128,128]{2,1,0:T(8,128)(2,1)} copy(bf16[64,128,128]{2,1,0:T(8,128)(2,1)} %get-tuple-element.31) | data formatting | bytes 4194304
  100.7 0.0 copy-done.1
  100.7 0.8 copy.15
  (1 shorter events, 0.0 us)
Async XLA Ops:
  0.6 12.3 %copy-start.2 = (bf16[3,3,128,128]{3,2,1,0:T(8,128)(2,1)S(1)}, bf16[3,3,128,128]{3,2,1,0:T(8,128)(2,1)}, u32[]{:S(2)}) copy-start(bf16[3,3,128,128]{3,2,1,0:T(8,128)(2,1)} %param.15) | copy-start | bytes 884740
  5.6 25.0 %all-to-all-start = ((bf16[32,72,128]{2,1,0:T(8,128)(2,1)}), bf16[32,72,128]{2,1,0:T(8,128)(2,1)S(1)}, u32[]{:S(2)}, u32[]{:S(2)}) async-start(bf16[32,72,128]{2,1,0:T(8,128)(2,1)} %pack.1), calls=%async_computation | async-start | bytes 1179648 | tf_op jit(solution)/shard_map/all_to_all | solution.py:381
  30.6 3.7 %copy-start = (bf16[32,72,128]{2,1,0:T(8,128)(2,1)}, bf16[32,72,128]{2,1,0:T(8,128)(2,1)S(1)}, u32[]{:S(2)}) copy-start(bf16[32,72,128]{2,1,0:T(8,128)(2,1)S(1)} %all-to-all-done.msg_ref) | copy-start | bytes 1769476
  97.5 3.2 %copy-start.1 = (f32[1152,128]{1,0:T(8,128)S(1)}, f32[1152,128]{1,0:T(8,128)}, u32[]{:S(2)}) copy-start(f32[1152,128]{1,0:T(8,128)} %get-tuple-element.23) | copy-start | bytes 1769476

commit v3 on v2

--- a/solution.py
+++ b/solution.py
@@ -17,13 +17,43 @@
 bf16 = jnp.bfloat16
 
 
-def pack_kernel(capacity, live_ref, rows_ref, owner_ref, lat_ref, lon_ref, pos_ref, out_ref):
+def pack_kernel(
+    capacity,
+    lat_total,
+    lon_total,
+    live_ref,
+    rows_ref,
+    owner_ref,
+    lat_ref,
+    lon_ref,
+    pos_ref,
+    out_ref,
+    held,
+    tally,
+    send_sem,
+    recv_sem,
+):
     devices = out_ref.shape[0]
-    row_total = rows_ref.shape[0]
+    row_total, channels = rows_ref.shape
+    me = lax.axis_index("lat") * lon_total + lax.axis_index("lon")
+
+    def place(peer):
+        return (peer // lon_total, peer % lon_total)
+
+    barrier = pltpu.get_barrier_semaphore()
+
+    def greet(k, _):
+        pl.semaphore_signal(
+            barrier, inc=1, device_id=place((me + k) % devices), device_id_type=pl.DeviceIdType.MESH
+        )
+        return 0
+
+    lax.fori_loop(1, devices, greet, 0)
     live = lax.broadcasted_iota(jnp.int32, (1, row_total), 1) < live_ref[0]
     owner = jnp.where(live, owner_ref[...], devices)
     match = lax.broadcasted_iota(jnp.int32, (devices, row_total), 0) == owner
     match = jnp.where(match, 1.0, 0.0)
+    tally[...] = jnp.broadcast_to(jnp.sum(match, axis=1, keepdims=True), tally.shape)
     upper = lax.broadcasted_iota(jnp.int32, (row_total, row_total), 0) < lax.broadcasted_iota(
         jnp.int32, (row_total, row_total), 1
     )
@@ -36,34 +66,80 @@
             pos_ref[...].astype(f32),
             lat_ref[...].astype(f32),
             lon_ref[...].astype(f32),
-            jnp.where(live, 1.0, 0.0),
-            jnp.zeros((geom_rows - 5, row_total), f32),
+            jnp.zeros((geom_rows - 4, row_total), f32),
         ],
         axis=0,
     ).astype(bf16)
-    group = max(1, min(devices, 256 // capacity))
+    group = math.gcd(devices, max(1, 256 // capacity))
+    groups = devices // group
     line = lax.broadcasted_iota(jnp.int32, (group * capacity, row_total), 0)
-    for first in range(0, devices, group):
+    row_line = lax.broadcasted_iota(jnp.int32, (geom_rows, capacity), 0)
+
+    def build(first):
         hit = jnp.where(line == slot - first * capacity, 1.0, 0.0).astype(bf16)
         placed = jnp.dot(hit, rows_ref[...], preferred_element_type=f32).astype(bf16)
         info = lax.dot_general(
             geometry, hit, (((1,), (1,)), ((), ())), preferred_element_type=f32
-        ).astype(bf16)
+        )
         for i in range(group):
-            out_ref[first + i, 0:capacity, :] = placed[i * capacity : (i + 1) * capacity]
-            out_ref[first + i, capacity : capacity + geom_rows, 0:capacity] = info[
-                :, i * capacity : (i + 1) * capacity
-            ]
+            held[first + i, 0:capacity, :] = placed[i * capacity : (i + 1) * capacity]
+            held[first + i, capacity : capacity + geom_rows, 0:capacity] = jnp.where(
+                row_line == 4,
+                tally[pl.ds(first + i, 1), 0:capacity],
+                info[:, i * capacity : (i + 1) * capacity],
+            ).astype(bf16)
+
+    def copy_to(peer, slot_at):
+        return pltpu.make_async_remote_copy(
+            src_ref=held.at[peer],
+            dst_ref=out_ref.at[slot_at],
+            send_sem=send_sem.at[peer],
+            recv_sem=recv_sem.at[slot_at],
+            device_id=place(peer),
+            device_id_type=pl.DeviceIdType.MESH,
+        )
+
+    def send(first):
+        for i in range(group):
+            peer = first + i
+
+            @pl.when(peer != me)
+            def _():
+                copy_to(peer, me).start()
+
+    odd = groups // 2
+
+    def first_of(k):
+        ahead = jnp.where(k < odd, 2 * k + 1, 2 * (k - odd))
+        return ((me // group + ahead) % groups) * group
+
+    build(first_of(0))
+    pl.semaphore_wait(barrier, devices - 1)
+
+    def work(k, _):
+        build(first_of(k))
+        send(first_of(k - 1))
+        return 0
+
+    lax.fori_loop(1, groups, work, 0)
+    send(first_of(groups - 1))
+    out_ref[me] = held[me]
+
+    def each(fn):
+        def body(k, _):
+            fn((me + k) % devices)
+            return 0
+
+        lax.fori_loop(1, devices, body, 0)
+
+    each(lambda peer: copy_to(peer, peer).wait_recv())
+    each(lambda peer: copy_to(peer, me).wait_send())
 
 
 def scatter_kernel(
     capacity,
     lanes,
-    count_ref,
-    lat_ref,
-    lon_ref,
-    fa_ref,
-    fb_ref,
+    info_ref,
     msg_ref,
     own_ref,
     up_ref,
@@ -78,6 +154,7 @@
     block,
 ):
     sources = msg_ref.shape[0]
+    slots = sources * capacity
     rows, cols = own_ref.shape[0], own_ref.shape[1]
     tall = canvas.shape[1]
     inv = 1.0 / (2.0 * rbf_scale * rbf_scale)
@@ -94,16 +171,24 @@
     def source(src, _):
         block[...] = msg_ref[src, 0:capacity, :].astype(f32)
 
-        def step(i, _):
+        def prepare(i):
             terms = []
             for j in range(lanes):
                 s = i * lanes + j
                 at = src * capacity + s
-                fa = fa_ref[at]
-                d = line - fb_ref[at]
+                fa, fb = info_ref[at], info_ref[at + slots]
+                d = line - fb
                 t = jnp.exp(-(d * d + (before + fa) * (before + fa)) * inv) * block[pl.ds(s, 1), :]
                 g = jnp.exp(jnp.full(t.shape, 2.0 * inv, f32) * fa)
-                terms.append((lat_ref[at], lon_ref[at], t, g))
+                r = info_ref[at + 2 * slots].astype(jnp.int32)
+                c = info_ref[at + 3 * slots].astype(jnp.int32)
+                terms.append((r, c, t, g))
+            return tuple(terms)
+
+        trips = (info_ref[4 * slots + src * capacity].astype(jnp.int32) + lanes - 1) // lanes
+
+        def step(i, terms):
+            ahead = prepare(jnp.minimum(i + 1, trips - 1))
             sums = []
             for j, (r, c, t, g) in enumerate(terms):
                 for a in range(taps):
@@ -112,9 +197,9 @@
             for j, (r, c, _, _) in enumerate(terms):
                 for a in range(taps):
                     canvas[j, r + a, pl.ds(c, taps), :] = sums[j * taps + a]
-            return 0
-
-        lax.fori_loop(0, (count_ref[src] + lanes - 1) // lanes, step, 0)
+            return ahead
+
+        lax.fori_loop(0, trips, step, prepare(0))
         return 0
 
     lax.fori_loop(0, sources, source, 0)
@@ -285,18 +370,36 @@
         return 0
 
     lax.fori_loop(0, devices, cut, 0)
-    part = math.gcd(tile_lat, 8)
-    strides = tile_lat // part
+    part = math.gcd(tile_lat // 2, 8)
+    strides = tile_lat // 2 // part
     half = strides // 2
 
     def apply(k, _):
-        acc = jnp.zeros((part * tile_lon, channels), f32)
-        for a in range(3):
-            start = pl.multiple_of((k * part + 2 - a) * tile_lon, tile_lon)
-            acc = acc + jnp.dot(
-                windows[pl.ds(start, part * tile_lon), :], weight_ref[a], preferred_element_type=f32
-            )
-        ig_ref[pl.ds(k * part, part)] = acc.reshape(part, tile_lon, channels).astype(bf16)
+        lhs = jnp.concatenate(
+            [
+                jnp.concatenate(
+                    [
+                        windows[
+                            pl.ds(
+                                pl.multiple_of((2 * (k * part + j) + r) * tile_lon, tile_lon),
+                                tile_lon,
+                            ),
+                            :,
+                        ]
+                        for r in range(4)
+                    ],
+                    axis=1,
+                )
+                for j in range(part)
+            ],
+            axis=0,
+        )
+        acc = jnp.dot(lhs, weight_ref[...], preferred_element_type=f32).astype(bf16)
+        for j in range(part):
+            for r in range(2):
+                ig_ref[2 * (k * part + j) + r] = acc[
+                    j * tile_lon : (j + 1) * tile_lon, r * channels : (r + 1) * channels
+                ]
         return 0
 
     def scattered(peer, slot):
@@ -362,13 +465,22 @@
     capacity = max(2, 2 * row_total // device_total)
     smem = pl.BlockSpec(memory_space=pltpu.SMEM)
     vmem = pl.BlockSpec(memory_space=pltpu.VMEM)
-    axes = ("lat", "lon")
-
-    outgoing = pl.pallas_call(
-        functools.partial(pack_kernel, capacity),
-        out_shape=jax.ShapeDtypeStruct((device_total, capacity + geom_rows, channels), bf16),
+
+    message = (device_total, capacity + geom_rows, channels)
+    incoming = pl.pallas_call(
+        functools.partial(pack_kernel, capacity, lat_total, lon_total),
+        out_shape=jax.ShapeDtypeStruct(message, bf16),
         in_specs=[smem] + [vmem] * 5,
         out_specs=vmem,
+        scratch_shapes=[
+            pltpu.VMEM(message, bf16),
+            pltpu.VMEM((device_total, channels), f32),
+            pltpu.SemaphoreType.DMA((device_total,)),
+            pltpu.SemaphoreType.DMA((device_total,)),
+        ],
+        compiler_params=pltpu.CompilerParams(
+            vmem_limit_bytes=24 * 2**20, collective_id=1, has_side_effects=True
+        ),
         name="pack",
     )(
         live_count,
@@ -378,10 +490,8 @@
         lon_offset.reshape(1, row_total),
         position.T,
     )
-    incoming = lax.all_to_all(outgoing, axes, split_axis=0, concat_axis=0, tiled=True)
-    info = incoming[:, capacity : capacity + 5, :capacity].astype(f32).transpose(1, 0, 2)
-    counts = jnp.sum(info[4], axis=1).astype(jnp.int32)
-    info = info.reshape(5, -1)
+    info = incoming[:, capacity : capacity + 5, :capacity].transpose(1, 0, 2).astype(f32)
+    info = info.reshape(-1)
 
     rows, cols = tile_lat + 2, tile_lon + 2
     tall = tile_lat + taps - 1
@@ -404,23 +514,27 @@
             jax.ShapeDtypeStruct(shape + (channels,), bf16)
             for shape in [(rows, cols)] + strip_shapes
         ],
-        in_specs=[smem] * 5 + [vmem],
+        in_specs=[smem, vmem],
         out_specs=[vmem] * 9,
         scratch_shapes=[
             pltpu.VMEM((lanes, tall, wide, channels), f32),
             pltpu.VMEM((capacity, channels), f32),
         ],
-        compiler_params=pltpu.CompilerParams(vmem_limit_bytes=60 * 2**20),
+        compiler_params=pltpu.CompilerParams(vmem_limit_bytes=32 * 2**20),
         name="scatter",
     )(
-        counts,
-        info[2].astype(jnp.int32),
-        info[3].astype(jnp.int32),
-        info[0],
-        info[1],
+        info,
         incoming,
     )
     kernel_t = conv_weight.transpose(0, 1, 3, 2).reshape(3, 3 * channels, channels)
+    none = jnp.zeros_like(kernel_t[0])
+    kernel_t = jnp.concatenate(
+        [
+            jnp.concatenate([kernel_t[2], kernel_t[1], kernel_t[0], none], axis=0),
+            jnp.concatenate([none, kernel_t[2], kernel_t[1], kernel_t[0]], axis=0),
+        ],
+        axis=1,
+    )
     flat_rows = 9 * channels
     share = flat_rows // device_total
     ring = pltpu.VMEM((device_total, share, channels), bf16)
@@ -451,7 +565,7 @@
             pltpu.SemaphoreType.DMA((device_total,)),
         ],
         compiler_params=pltpu.CompilerParams(
-            vmem_limit_bytes=60 * 2**20, collective_id=0, has_side_effects=True
+            vmem_limit_bytes=36 * 2**20, collective_id=0, has_side_effects=True
         ),
         name="conv",
     )(own, *strips, features, kernel_t)

time: 102 us -> 90.5 us (0.89)
  waiting for transfers between devices: 16.7 us -> 0 us
  Pallas kernels: 67.5 us -> 82.6 us
  starting transfers between devices: 7.33 us -> 0 us
  local copies, waits for them, and re-layouts: 7.6 us -> 6.25 us
    pallas_call x1, Pallas kernels: 4.29 us -> 21.6 us  [shards(): pl.pallas_call(functools.partial(pack_kernel, capacity, lat_total, lon_to...]
    all_to_all x1 -> x0, waiting for transfers between devices: 16.7 us -> none  [shards(): lax.all_to_all(outgoing, axes, split_axis=0, concat_axis=0, tiled=True)]
    all_to_all x1 -> x0, starting transfers between devices: 7.33 us -> none  [shards(): lax.all_to_all(outgoing, axes, split_axis=0, concat_axis=0, tiled=True)]
    pallas_call x1, Pallas kernels: 17.7 us -> 10.4 us  [shards(): pl.pallas_call(functools.partial(scatter_kernel, capacity, lanes), out_sh...]
    pallas_call x1, Pallas kernels: 45.5 us -> 50.6 us  [shards(): pl.pallas_call(functools.partial(conv_kernel, lat_total, lon_total), out_...]
    reshape x0 -> x2, local copies, waits for them, and re-layouts: none -> 1.61 us  [shards(): info = info.reshape(-1)]
    slice x0 -> x4, local copies, waits for them, and re-layouts: none -> 1.39 us  [the longest x2 1.13 us: shards(): kernel_t[2]]
    squeeze x2 -> x0, local copies, waits for them, and re-layouts: 1.33 us -> none  [the longest x1 0.67 us: shards(): info[1]]
  transfers between devices with their start and end apart: 1 -> 0, of which waited for: 1 -> 0; matrix products, arithmetic and copies ran while one was open for 1% -> 0% of each run, Pallas kernels for 0% -> 0%
where the time goes in v3:
time: 90.5 us; the launch traced here: 90.4 us
  Pallas kernels  82.6 us (91%)
  local copies, waits for them, and re-layouts  6.25 us (7%)
  between operations  1.46 us (2%)
    pallas_call x1, Pallas kernels, shards(): pl.pallas_call(functools.partial(conv_kernel, lat_total, lon_total), out_...  50.6 us
    pallas_call x1, Pallas kernels, shards(): pl.pallas_call(functools.partial(pack_kernel, capacity, lat_total, lon_to...  21.6 us
    pallas_call x1, Pallas kernels, shards(): pl.pallas_call(functools.partial(scatter_kernel, capacity, lanes), out_sh...  10.4 us
    unnamed x14, local copies, waits for them, and re-layouts  3.23 us

profile of v3, /device:TPU:0, one launch (start us, length us, event | category | flops | bytes accessed | tf_op | source)
XLA Modules:
  0.0 90.4 jit_solution(10887605498488261195)
XLA Ops:
  0.6 0.0 copy-start.5
  0.6 0.0 copy-start.4
  0.7 0.0 copy-start.3
  0.7 0.0 copy-start.2
  1.3 1.0 %fusion = (bf16[1,3,128,128]{2,3,1,0:T(8,128)(2,1)S(1)}, bf16[1,3,128,128]{2,3,1,0:T(8,128)(2,1)S(1)}, bf16[1,3,128,128]{2,3,1,0:T(8,128)(2,1)S(1)}) fusion(bf16[3,3,128,128]{2,3,1,0:T(8,128)(2,1)} %bitcast.19), kind=kLoop, calls=%fused_computation.2 | loop fusion | bytes 589824 | tf_op jit(solution)/shard_map/slice | solution.py:533
  2.4 0.1 copy.14
  2.5 0.1 copy.16
  2.6 0.1 copy.15
  2.8 0.0 copy-start
  2.8 0.1 maximum_maximum_fusion.refs_9_
  2.9 0.0 copy-done.5
  2.9 0.0 copy-done.4
  2.9 0.0 copy-done.3
  2.9 0.0 copy-done.2
  2.9 0.0 copy-start.1
  2.9 1.1 %copy-done.1 = bf16[1024,128]{1,0:T(8,128)(2,1)S(1)} copy-done((bf16[1024,128]{1,0:T(8,128)(2,1)S(1)}, bf16[1024,128]{1,0:T(8,128)(2,1)}, u32[]{:S(2)}) %copy-start.1) | copy-done | bytes 262168
  4.0 21.6 %pack.1.msg_ref = bf16[32,72,128]{2,1,0:T(8,128)(2,1)S(1)} custom-call(s32[1]{0:T(128)S(6)} %copy.19.live_ref, bf16[1024,128]{1,0:T(8,128)(2,1)S(1)} %copy-done.1, s32[1,1024]{1,0:T(1,128)S(1)} %bitcast.12, s32[1,1024]{1,0:T(1,128)S(1)} %bitcast.13, s32[1,1024]{1,0:T(1,128)S(1)} %bitcast.14, bf16[2,1024]{1,0:T(2,128)(2,1)S(1)} %bitcast.15), custom_call_target="tpu_custom_call" | custom-call | tf_op jit(solution)/shard_map/pack/pallas_call | solution.py:470
  25.6 0.7 copy.13
  26.2 1.0 %reshape.35.info_ref = f32[10240]{0:T(1024)S(1)} reshape(f32[5,32,64]{2,1,0:T(8,128)} %copy.13) | data formatting | bytes 81920 | tf_op jit(solution)/shard_map/reshape | solution.py:494
  27.2 10.4 %scatter.1 = (bf16[66,130,128]{2,1,0:T(8,128)(2,1)S(1)}, bf16[4,130,128]{2,1,0:T(8,128)(2,1)S(1)}, bf16[5,130,128]{2,1,0:T(8,128)(2,1)S(1)}, bf16[66,4,128]{2,1,...) custom-call(f32[10240]{0:T(1024)S(1)} %reshape.35.info_ref, ...), custom_call_target="tpu_custom_call" | custom-call | tf_op jit(solution)/shard_map/scatter/pallas_call | solution.py:511
  37.6 0.0 copy-done
  37.6 50.6 %conv.1 = (bf16[64,128,128]{2,1,0:T(8,128)(2,1)S(1)}, f32[1152,128]{1,0:T(8,128)S(1)}) custom-call(bf16[66,130,128]{2,1,0:T(8,128)(2,1)S(1)} %get-tuple-element.13.own_ref, bf16[4,130,128]{2,1,0:T(8,128)(2,1)S(1)} %get-tuple-element.14.refs_0_, bf16[5,130,128]{2,1,0:T(8,128)(2,1)S(1)} %get-tuple-element.15.refs_1_, ...), custom_call_target="tpu_custom_call" | custom-call | tf_op jit(solution)/shard_map/conv/pallas_call | solution.py:541
  88.3 1.3 %copy.20 = bf16[64,128,128]{2,1,0:T(8,128)(2,1)} copy(bf16[64,128,128]{2,1,0:T(8,128)(2,1)S(1)} %get-tuple-element.29) | data formatting | bytes 4194304
  89.6 0.8 copy.21
  (2 shorter events, 0.0 us)
Async XLA Ops:
  0.6 2.2 %copy-start.5 = (bf16[1024,2]{0,1:T(2,128)(2,1)S(1)}, bf16[1024,2]{0,1:T(2,128)(2,1)}, u32[]{:S(2)}) copy-start(bf16[1024,2]{0,1:T(2,128)(2,1)} %param.12) | copy-start | bytes 12292
  0.6 2.2 %copy-start.4 = (s32[1024]{0:T(1024)S(1)}, s32[1024]{0:T(1024)}, u32[]{:S(2)}) copy-start(s32[1024]{0:T(1024)} %param.11) | copy-start | bytes 12292
  0.7 2.2 %copy-start.3 = (s32[1024]{0:T(1024)S(1)}, s32[1024]{0:T(1024)}, u32[]{:S(2)}) copy-start(s32[1024]{0:T(1024)} %param.10) | copy-start | bytes 12292
  0.7 2.2 %copy-start.2 = (s32[1024,1]{0,1:T(1,128)S(1)}, s32[1024,1]{0,1:T(1,128)}, u32[]{:S(2)}) copy-start(s32[1024,1]{0,1:T(1,128)} %param.9) | copy-start | bytes 12292
  2.8 34.8 %copy-start = (bf16[64,128,128]{2,1,0:T(8,128)(2,1)S(1)}, bf16[64,128,128]{2,1,0:T(8,128)(2,1)}, u32[]{:S(2)}) copy-start(bf16[64,128,128]{2,1,0:T(8,128)(2,1)} %refs_8_.1) | copy-start | bytes 6291460
  2.9 1.1 %copy-start.1 = (bf16[1024,128]{1,0:T(8,128)(2,1)S(1)}, bf16[1024,128]{1,0:T(8,128)(2,1)}, u32[]{:S(2)}) copy-start(bf16[1024,128]{1,0:T(8,128)(2,1)} %rows_ref.1) | copy-start | bytes 786436

commit v4 on v3

--- a/solution.py
+++ b/solution.py
@@ -243,14 +243,17 @@
 ):
     strips, (feat_ref, weight_ref, ig_ref, wg_ref) = refs[:8], refs[8:12]
     landed = refs[12:20]
-    (grid, windows, turned, total, flat, pieces, parts, mine, gathered) = refs[20:29]
-    halo_send, halo_recv, part_send, part_recv, all_send, all_recv = refs[29:]
+    (grid, windows, turned, total, flat, mixer, pieces, twin, parts, mine, gathered) = refs[20:31]
+    halo_send, halo_recv, pair_send, pair_recv, part_send, part_recv, all_send, all_recv = refs[31:]
     rows, cols = own_ref.shape[0], own_ref.shape[1]
     tile_lat, tile_lon, channels = feat_ref.shape
     up, down = before + 1, after + 1
     devices = lat_total * lon_total
     lat, lon = lax.axis_index("lat"), lax.axis_index("lon")
     me = lat * lon_total + lon
+    chips = devices // 2
+    core, chip = me % 2, me // 2
+    other = 1 - core
 
     def place(peer):
         return (peer // lon_total, peer % lon_total)
@@ -304,6 +307,13 @@
         return 0
 
     lax.fori_loop(0, tile_lat, turn, 0)
+    mixer[...] = jnp.zeros_like(mixer)
+    for a in range(3):
+        for b in range(3):
+            tap = weight_ref[a, b].T
+            for r in range(2):
+                at = ((r + 2 - a) * 3 + b) * channels
+                mixer[at : at + channels, r * channels : (r + 1) * channels] = tap
     total[...] = jnp.zeros_like(total)
 
     for (copy, _, takes), (da, db), ref in zip(halos, ways, landed):
@@ -372,7 +382,7 @@
     lax.fori_loop(0, devices, cut, 0)
     part = math.gcd(tile_lat // 2, 8)
     strides = tile_lat // 2 // part
-    half = strides // 2
+    first, second = strides // 4, strides * 3 // 4
 
     def apply(k, _):
         lhs = jnp.concatenate(
@@ -394,7 +404,7 @@
             ],
             axis=0,
         )
-        acc = jnp.dot(lhs, weight_ref[...], preferred_element_type=f32).astype(bf16)
+        acc = jnp.dot(lhs, mixer[...], preferred_element_type=f32).astype(bf16)
         for j in range(part):
             for r in range(2):
                 ig_ref[2 * (k * part + j) + r] = acc[
@@ -402,58 +412,86 @@
                 ]
         return 0
 
+    def paired(src, dst, n):
+        return pltpu.make_async_remote_copy(
+            src_ref=src,
+            dst_ref=dst,
+            send_sem=pair_send.at[n],
+            recv_sem=pair_recv.at[n],
+            device_id=place(chip * 2 + other),
+            device_id_type=pl.DeviceIdType.MESH,
+        )
+
     def scattered(peer, slot):
         return pltpu.make_async_remote_copy(
-            src_ref=pieces.at[peer],
+            src_ref=pieces.at[core * chips + peer],
             dst_ref=parts.at[slot],
             send_sem=part_send.at[peer],
             recv_sem=part_recv.at[slot],
-            device_id=place(peer),
+            device_id=place(peer * 2 + core),
             device_id_type=pl.DeviceIdType.MESH,
         )
 
     def shared(peer, slot):
         return pltpu.make_async_remote_copy(
             src_ref=mine,
-            dst_ref=gathered.at[slot],
+            dst_ref=gathered.at[core * chips + slot],
             send_sem=all_send.at[peer],
             recv_sem=all_recv.at[slot],
-            device_id=place(peer),
+            device_id=place(peer * 2 + core),
             device_id_type=pl.DeviceIdType.MESH,
         )
 
     def each(fn):
         def body(k, _):
-            fn((me + k) % devices)
+            fn((chip + k) % chips)
             return 0
 
-        lax.fori_loop(1, devices, body, 0)
-
-    each(lambda peer: scattered(peer, me).start())
-    lax.fori_loop(0, half, apply, 0)
+        lax.fori_loop(1, chips, body, 0)
+
+    swap = paired(pieces.at[pl.ds(other * chips, chips)], twin, 0)
+    swap.start()
+    lax.fori_loop(0, first, apply, 0)
+    swap.wait_recv()
+
+    def merge(p, _):
+        at = core * chips + p
+        pieces[at] = (flat[pl.ds(at * share, share), :] + twin[p].astype(f32)).astype(bf16)
+        return 0
+
+    lax.fori_loop(0, chips, merge, 0)
+    each(lambda peer: scattered(peer, chip).start())
+    lax.fori_loop(first, second, apply, 0)
+    parts[chip] = pieces[core * chips + chip]
     each(lambda peer: scattered(peer, peer).wait_recv())
-    parts[me] = pieces[me]
-
-    def gather_sum(d, acc):
-        return acc + parts[d].astype(f32)
+
+    def gather_sum(p, acc):
+        return acc + parts[p].astype(f32)
 
     mine[...] = lax.fori_loop(
-        0, devices, gather_sum, jnp.zeros((share, channels), f32)
+        0, chips, gather_sum, jnp.zeros((share, channels), f32)
     ).astype(bf16)
-    each(lambda peer: shared(peer, me).start())
-    lax.fori_loop(half, strides, apply, 0)
+    each(lambda peer: shared(peer, chip).start())
+    gathered[core * chips + chip] = mine[...]
+    lax.fori_loop(second, strides, apply, 0)
     each(lambda peer: shared(peer, peer).wait_recv())
-    gathered[me] = mine[...]
+    held = gathered.at[pl.ds(core * chips, chips)]
+    back = paired(held, held, 1)
+    back.start()
 
     def spill(d, _):
         wg_ref[pl.ds(d * share, share), :] = gathered[d].astype(f32)
         return 0
 
-    lax.fori_loop(0, devices, spill, 0)
+    lax.fori_loop(core * chips, (core + 1) * chips, spill, 0)
+    back.wait_recv()
+    lax.fori_loop(other * chips, (other + 1) * chips, spill, 0)
     for (copy, sends, _), (da, _) in zip(halos, ways):
         when(da, sends, copy.wait_send)
-    each(lambda peer: scattered(peer, me).wait_send())
-    each(lambda peer: shared(peer, me).wait_send())
+    swap.wait_send()
+    back.wait_send()
+    each(lambda peer: scattered(peer, chip).wait_send())
+    each(lambda peer: shared(peer, chip).wait_send())
 
 
 def shards(grad_rows, owner, lat_offset, lon_offset, position, live_count, features, conv_weight):
@@ -526,18 +564,10 @@
         info,
         incoming,
     )
-    kernel_t = conv_weight.transpose(0, 1, 3, 2).reshape(3, 3 * channels, channels)
-    none = jnp.zeros_like(kernel_t[0])
-    kernel_t = jnp.concatenate(
-        [
-            jnp.concatenate([kernel_t[2], kernel_t[1], kernel_t[0], none], axis=0),
-            jnp.concatenate([none, kernel_t[2], kernel_t[1], kernel_t[0]], axis=0),
-        ],
-        axis=1,
-    )
     flat_rows = 9 * channels
     share = flat_rows // device_total
     ring = pltpu.VMEM((device_total, share, channels), bf16)
+    half_ring = pltpu.VMEM((device_total // 2, share, channels), bf16)
     input_grad, weight_grad = pl.pallas_call(
         functools.partial(conv_kernel, lat_total, lon_total),
         out_shape=[
@@ -553,22 +583,26 @@
             pltpu.VMEM((channels, (rows + 2) * tile_lon), bf16),
             pltpu.VMEM((3 * channels, 3 * channels), f32),
             pltpu.VMEM((flat_rows, channels), f32),
+            pltpu.VMEM((4 * 3 * channels, 2 * channels), bf16),
             ring,
-            ring,
+            half_ring,
+            half_ring,
             pltpu.VMEM((share, channels), bf16),
             ring,
             pltpu.SemaphoreType.DMA((8,)),
             pltpu.SemaphoreType.DMA((8,)),
-            pltpu.SemaphoreType.DMA((device_total,)),
-            pltpu.SemaphoreType.DMA((device_total,)),
-            pltpu.SemaphoreType.DMA((device_total,)),
-            pltpu.SemaphoreType.DMA((device_total,)),
+            pltpu.SemaphoreType.DMA((2,)),
+            pltpu.SemaphoreType.DMA((2,)),
+            pltpu.SemaphoreType.DMA((device_total // 2,)),
+            pltpu.SemaphoreType.DMA((device_total // 2,)),
+            pltpu.SemaphoreType.DMA((device_total // 2,)),
+            pltpu.SemaphoreType.DMA((device_total // 2,)),
         ],
         compiler_params=pltpu.CompilerParams(
             vmem_limit_bytes=36 * 2**20, collective_id=0, has_side_effects=True
         ),
         name="conv",
-    )(own, *strips, features, kernel_t)
+    )(own, *strips, features, conv_weight)
     return input_grad, weight_grad.reshape(3, 3, channels, channels)
 
 

time: 90.5 us -> 86.7 us (0.958)
  Pallas kernels: 82.6 us -> 77.3 us
  local copies, waits for them, and re-layouts: 6.25 us -> 7.51 us
    pallas_call x1, Pallas kernels: 50.6 us -> 45.5 us  [shards(): pl.pallas_call(functools.partial(conv_kernel, lat_total, lon_total), out_...]
    unnamed x14 -> x16, local copies, waits for them, and re-layouts: 3.23 us -> 7.41 us
    reshape x2, local copies, waits for them, and re-layouts: 1.61 us -> 0.09 us  [shards(): info = info.reshape(-1)]
    slice x4 -> x0, local copies, waits for them, and re-layouts: 1.39 us -> none  [the longest x2 1.13 us: shards(): kernel_t[2]]
where the time goes in v4:
time: 86.7 us; the launch traced here: 86.2 us
  Pallas kernels  77.3 us (89%)
  local copies, waits for them, and re-layouts  7.51 us (9%)
  between operations  1.4 us (2%)
    pallas_call x1, Pallas kernels, shards(): pl.pallas_call(functools.partial(conv_kernel, lat_total, lon_total), out_...  45.5 us
    pallas_call x1, Pallas kernels, shards(): pl.pallas_call(functools.partial(pack_kernel, capacity, lat_total, lon_to...  21.6 us
    pallas_call x1, Pallas kernels, shards(): pl.pallas_call(functools.partial(scatter_kernel, capacity, lanes), out_sh...  10.1 us
    unnamed x16, local copies, waits for them, and re-layouts  7.41 us

profile of v4, /device:TPU:0, one launch (start us, length us, event | category | flops | bytes accessed | tf_op | source)
XLA Modules:
  0.0 86.2 jit_solution(7736202530238172738)
XLA Ops:
  0.6 0.0 copy-start.1
  1.3 0.0 copy-start.2
  1.3 0.9 %copy-done.2 = bf16[1024,128]{1,0:T(8,128)(2,1)S(1)} copy-done((bf16[1024,128]{1,0:T(8,128)(2,1)S(1)}, bf16[1024,128]{1,0:T(8,128)(2,1)}, u32[]{:S(2)}) %copy-start.2) | copy-done | bytes 262168
  2.3 0.0 copy-start.3
  2.3 0.7 copy-done.3
  3.0 0.0 copy-start.4
  3.0 0.7 copy-done.4
  3.7 0.0 copy-start.5
  3.7 0.7 copy-done.5
  4.3 0.0 copy-start.6
  4.3 0.7 copy-done.6
  5.0 21.6 %pack.1.msg_ref = bf16[32,72,128]{2,1,0:T(8,128)(2,1)S(1)} custom-call(s32[1]{0:T(128)S(6)} %copy.13.live_ref, bf16[1024,128]{1,0:T(8,128)(2,1)S(1)} %copy-done.2, s32[1,1024]{1,0:T(1,128)S(1)} %bitcast.8, s32[1,1024]{1,0:T(1,128)S(1)} %bitcast.9, s32[1,1024]{1,0:T(1,128)S(1)} %bitcast.10, bf16[2,1024]{1,0:T(2,128)(2,1)S(1)} %bitcast.11), custom_call_target="tpu_custom_call" | custom-call | tf_op jit(solution)/shard_map/pack/pallas_call | solution.py:508
  26.7 0.1 reshape.28.info_ref
  26.8 10.1 %scatter.1 = (bf16[66,130,128]{2,1,0:T(8,128)(2,1)S(1)}, bf16[4,130,128]{2,1,0:T(8,128)(2,1)S(1)}, bf16[5,130,128]{2,1,0:T(8,128)(2,1)S(1)}, bf16[66,4,128]{2,1,...) custom-call(f32[10240]{0:T(1024)S(1)} %reshape.28.info_ref, ...), custom_call_target="tpu_custom_call" | custom-call | tf_op jit(solution)/shard_map/scatter/pallas_call | solution.py:549
  36.9 0.0 copy-done.1
  36.9 0.0 copy-start
  36.9 1.6 %copy-done = bf16[64,128,128]{2,1,0:T(8,128)(2,1)S(1)} copy-done((bf16[64,128,128]{2,1,0:T(8,128)(2,1)S(1)}, bf16[64,128,128]{2,1,0:T(8,128)(2,1)}, u32[]{:S(2)}) %copy-start) | copy-done | bytes 2097176
  38.5 45.5 %conv.1 = (bf16[64,128,128]{2,1,0:T(8,128)(2,1)S(1)}, f32[1152,128]{1,0:T(8,128)S(1)}) custom-call(bf16[66,130,128]{2,1,0:T(8,128)(2,1)S(1)} %get-tuple-element.13.own_ref, bf16[4,130,128]{2,1,0:T(8,128)(2,1)S(1)} %get-tuple-element.14.refs_0_, bf16[5,130,128]{2,1,0:T(8,128)(2,1)S(1)} %get-tuple-element.15.refs_1_, ...), custom_call_target="tpu_custom_call" | custom-call | tf_op jit(solution)/shard_map/conv/pallas_call | solution.py:571
  84.0 1.3 %copy.14 = bf16[64,128,128]{2,1,0:T(8,128)(2,1)} copy(bf16[64,128,128]{2,1,0:T(8,128)(2,1)S(1)} %get-tuple-element.26) | data formatting | bytes 4194304
  85.4 0.8 copy.15
  (2 shorter events, 0.0 us)
Async XLA Ops:
  0.6 36.3 %copy-start.1 = (bf16[3,3,128,128]{3,2,1,0:T(8,128)(2,1)S(1)}, bf16[3,3,128,128]{3,2,1,0:T(8,128)(2,1)}, u32[]{:S(2)}) copy-start(bf16[3,3,128,128]{3,2,1,0:T(8,128)(2,1)} %refs_9_.1) | copy-start | bytes 884740
  1.3 1.0 %copy-start.2 = (bf16[1024,128]{1,0:T(8,128)(2,1)S(1)}, bf16[1024,128]{1,0:T(8,128)(2,1)}, u32[]{:S(2)}) copy-start(bf16[1024,128]{1,0:T(8,128)(2,1)} %rows_ref.1) | copy-start | bytes 786436
  2.3 0.7 copy-start.3
  3.0 0.7 copy-start.4
  3.7 0.7 copy-start.5
  4.3 0.7 copy-start.6
  36.9 1.6 %copy-start = (bf16[64,128,128]{2,1,0:T(8,128)(2,1)S(1)}, bf16[64,128,128]{2,1,0:T(8,128)(2,1)}, u32[]{:S(2)}) copy-start(bf16[64,128,128]{2,1,0:T(8,128)(2,1)} %refs_8_.1) | copy-start | bytes 6291460

commit v5 on v4

--- a/solution.py
+++ b/solution.py
@@ -517,7 +517,7 @@
             pltpu.SemaphoreType.DMA((device_total,)),
         ],
         compiler_params=pltpu.CompilerParams(
-            vmem_limit_bytes=24 * 2**20, collective_id=1, has_side_effects=True
+            vmem_limit_bytes=60 * 2**20, collective_id=1, has_side_effects=True
         ),
         name="pack",
     )(

time: 86.7 us -> 88 us (1.015); the launches traced: 86.2 us -> 86.6 us
  local copies, waits for them, and re-layouts: 7.51 us -> 4.88 us
  Pallas kernels: 77.3 us -> 79.5 us
    unnamed x16 -> x8, local copies, waits for them, and re-layouts: 7.41 us -> 4.79 us
    pallas_call x1, Pallas kernels: 21.6 us -> 23.5 us  [shards(): pl.pallas_call(functools.partial(pack_kernel, capacity, lat_total, lon_to...]
where the time goes in v5:
time: 88 us; the launch traced here: 86.6 us
  Pallas kernels  79.5 us (90%)
  local copies, waits for them, and re-layouts  4.88 us (6%)
  between operations  1.39 us (2%)
    pallas_call x1, Pallas kernels, shards(): pl.pallas_call(functools.partial(conv_kernel, lat_total, lon_total), out_...  45.4 us
    pallas_call x1, Pallas kernels, shards(): pl.pallas_call(functools.partial(pack_kernel, capacity, lat_total, lon_to...  23.5 us
    pallas_call x1, Pallas kernels, shards(): pl.pallas_call(functools.partial(scatter_kernel, capacity, lanes), out_sh...  10.6 us
    unnamed x8, local copies, waits for them, and re-layouts  4.79 us

profile of v5, /device:TPU:0, one launch (start us, length us, event | category | flops | bytes accessed | tf_op | source)
XLA Modules:
  0.0 86.6 jit_solution(5583358598529232778)
XLA Ops:
  0.6 0.0 copy-start.2
  1.3 23.5 %pack.1.msg_ref = bf16[32,72,128]{2,1,0:T(8,128)(2,1)} custom-call(s32[1]{0:T(128)S(6)} %copy.13.live_ref, bf16[1024,128]{1,0:T(8,128)(2,1)} %rows_ref.1, s32[1,1024]{1,0:T(1,128)} %bitcast.8, s32[1,1024]{1,0:T(1,128)} %bitcast.9, s32[1,1024]{1,0:T(1,128)} %bitcast.10, bf16[2,1024]{1,0:T(2,128)(2,1)} %bitcast.11), custom_call_target="tpu_custom_call" | custom-call | tf_op jit(solution)/shard_map/pack/pallas_call | solution.py:508
  24.8 0.9 convert_bitcast_fusion
  25.7 0.1 reshape.28.info_ref
  25.8 0.0 copy-start
  25.8 1.1 %copy-done = bf16[32,72,128]{2,1,0:T(8,128)(2,1)S(1)} copy-done((bf16[32,72,128]{2,1,0:T(8,128)(2,1)S(1)}, bf16[32,72,128]{2,1,0:T(8,128)(2,1)}, u32[]{:S(2)}) %copy-start) | copy-done | bytes 589848
  26.8 10.6 %scatter.1 = (bf16[66,130,128]{2,1,0:T(8,128)(2,1)S(1)}, bf16[4,130,128]{2,1,0:T(8,128)(2,1)S(1)}, bf16[5,130,128]{2,1,0:T(8,128)(2,1)S(1)}, bf16[66,4,128]{2,1,...) custom-call(f32[10240]{0:T(1024)S(1)} %reshape.28.info_ref, ...), custom_call_target="tpu_custom_call" | custom-call | tf_op jit(solution)/shard_map/scatter/pallas_call | solution.py:549
  37.4 0.0 copy-done.2
  37.4 0.0 copy-start.1
  37.4 1.6 %copy-done.1 = bf16[64,128,128]{2,1,0:T(8,128)(2,1)S(1)} copy-done((bf16[64,128,128]{2,1,0:T(8,128)(2,1)S(1)}, bf16[64,128,128]{2,1,0:T(8,128)(2,1)}, u32[]{:S(2)}) %copy-start.1) | copy-done | bytes 2097176
  39.0 45.4 %conv.1 = (bf16[64,128,128]{2,1,0:T(8,128)(2,1)S(1)}, f32[1152,128]{1,0:T(8,128)S(1)}) custom-call(bf16[66,130,128]{2,1,0:T(8,128)(2,1)S(1)} %get-tuple-element.13.own_ref, bf16[4,130,128]{2,1,0:T(8,128)(2,1)S(1)} %get-tuple-element.14.refs_0_, bf16[5,130,128]{2,1,0:T(8,128)(2,1)S(1)} %get-tuple-element.15.refs_1_, ...), custom_call_target="tpu_custom_call" | custom-call | tf_op jit(solution)/shard_map/conv/pallas_call | solution.py:571
  84.4 1.3 %copy.14 = bf16[64,128,128]{2,1,0:T(8,128)(2,1)} copy(bf16[64,128,128]{2,1,0:T(8,128)(2,1)S(1)} %get-tuple-element.26) | data formatting | bytes 4194304
  85.8 0.8 copy.15
  (1 shorter events, 0.0 us)
Async XLA Ops:
  0.6 36.8 %copy-start.2 = (bf16[3,3,128,128]{3,2,1,0:T(8,128)(2,1)S(1)}, bf16[3,3,128,128]{3,2,1,0:T(8,128)(2,1)}, u32[]{:S(2)}) copy-start(bf16[3,3,128,128]{3,2,1,0:T(8,128)(2,1)} %refs_9_.1) | copy-start | bytes 884740
  25.8 1.1 %copy-start = (bf16[32,72,128]{2,1,0:T(8,128)(2,1)S(1)}, bf16[32,72,128]{2,1,0:T(8,128)(2,1)}, u32[]{:S(2)}) copy-start(bf16[32,72,128]{2,1,0:T(8,128)(2,1)} %pack.1.msg_ref) | copy-start | bytes 1769476
  37.4 1.6 %copy-start.1 = (bf16[64,128,128]{2,1,0:T(8,128)(2,1)S(1)}, bf16[64,128,128]{2,1,0:T(8,128)(2,1)}, u32[]{:S(2)}) copy-start(bf16[64,128,128]{2,1,0:T(8,128)(2,1)} %refs_8_.1) | copy-start | bytes 6291460
